TPU v7x, 32 devices: a whole 2x2x4 slice. The times are simulated.
32 devices in a mesh: gx: 8 (over z, core), gy: 2 (over x), ga: 2 (over y).
Axes of the slice: x: 2, y: 2, z: 4, core: 2. Of those that a mesh axis runs over, the one named last changes fastest.
Arguments:
- euler_table: float32 [3, 2048], replicated, may hold values from -3.140625 to 3.140625
- crystal: float32 [21], replicated, may hold values from -0.08 to 3.4
- orient: int32 [32, 8, 2, 512], P('ga', 'gx', 'gy'), may hold values from 0 to 2047
- weight: bfloat16 [32, 8, 2, 512], P('ga', 'gx', 'gy'), may hold values from 0.099609375 to 1
- cell_map: int32 [8, 2, 512], P('gx', 'gy'), may hold values from 0 to 511, each once within a row
- density: float32 [64, 8, 16], P('gx', 'gy', 'ga'), may hold values from 0.5 to 2
- velocity: float32 [3, 64, 8, 16], P(None, 'gx', 'gy', 'ga'), may hold values from -6 to 6
- stress: float32 [6, 64, 8, 16], P(None, 'gx', 'gy', 'ga'), may hold values from -6 to 6
Outputs:
- stiffness: float32 [21, 64, 8, 16], P(None, 'gx', 'gy', 'ga')
- final_velocity: float32 [3, 64, 8, 16], P(None, 'gx', 'gy', 'ga')
- final_stress: float32 [6, 64, 8, 16], P(None, 'gx', 'gy', 'ga')
Inputs may be any that keep to these rules, and one draw needn't show every extreme that they name: `cell_map`: each partition's row is a permutation of the 512 canonical indices.
All inputs are finite; a program needn't handle non-finite values.
Results may differ from a plain program's by a relative error of at most 0.0003.
Values sent between devices are 32-bit elements; how exact they have to be, the bound alone decides.
No kernel may reach another device: no remote copies, remote signals or barrier semaphores. Data moves between devices by JAX's collectives and lax.ppermute only.
A program may use at most 128 MiB of HBM per device.

v0:
```python
import jax
import jax.numpy as jnp
from jax import lax
from jax.sharding import PartitionSpec as P

STEPS = 2


stencil_weights = (0.8, -0.2, 4.0 / 105.0, -1.0 / 280.0)
time_step = 0.2
grain_block = 4
voigt_pairs = ((0, 0), (1, 1), (2, 2), (1, 2), (0, 2), (0, 1))
upper_pairs = [
    (row_index, col_index) for row_index in range(6) for col_index in range(row_index, 6)
]


def with_halo(cells, sides, width):
    for axis, dim in sides:
        count = lax.axis_size(axis)
        ends = count - 1
        head = lax.slice_in_dim(cells, 0, width, axis=dim)
        tail = lax.slice_in_dim(cells, cells.shape[dim] - width, cells.shape[dim], axis=dim)
        cells = jnp.concatenate(
            [
                lax.ppermute(tail, axis, [(i, (i + 1) % count) for i in range(ends)]),
                cells,
                lax.ppermute(head, axis, [((i + 1) % count, i) for i in range(ends)]),
            ],
            axis=dim,
        )
    return cells


def symmetric_index(first_index, second_index):
    return upper_pairs.index((min(first_index, second_index), max(first_index, second_index)))


def ordered_sum(summands):
    running = summands[0]
    for summand in summands[1:]:
        running = running + summand
    return running


def rotated_table(euler_table, crystal):
    cos_one, sin_one = (jnp.cos(euler_table[0]), jnp.sin(euler_table[0]))
    cos_mid, sin_mid = (jnp.cos(euler_table[1]), jnp.sin(euler_table[1]))
    cos_two, sin_two = (jnp.cos(euler_table[2]), jnp.sin(euler_table[2]))
    bunge = [
        [
            cos_one * cos_two - sin_one * sin_two * cos_mid,
            sin_one * cos_two + cos_one * sin_two * cos_mid,
            sin_two * sin_mid,
        ],
        [
            -cos_one * sin_two - sin_one * cos_two * cos_mid,
            -sin_one * sin_two + cos_one * cos_two * cos_mid,
            cos_two * sin_mid,
        ],
        [sin_one * sin_mid, -cos_one * sin_mid, cos_mid],
    ]
    rotation = [[bunge[col_index][row_index] for col_index in range(3)] for row_index in range(3)]
    bond = []
    for out_index in range(6):
        first, second = voigt_pairs[out_index]
        bond_row = []
        for in_index in range(6):
            third, fourth = voigt_pairs[in_index]
            if in_index < 3:
                bond_row.append(rotation[first][third] * rotation[second][third])
            else:
                bond_row.append(
                    rotation[first][third] * rotation[second][fourth]
                    + rotation[first][fourth] * rotation[second][third]
                )
        bond.append(bond_row)
    entries = [
        [crystal[symmetric_index(row_index, col_index)] for col_index in range(6)]
        for row_index in range(6)
    ]
    product = [
        [
            ordered_sum([bond[row_index][inner] * entries[inner][col_index] for inner in range(6)])
            for col_index in range(6)
        ]
        for row_index in range(6)
    ]
    rotated = [
        ordered_sum([product[row_index][inner] * bond[col_index][inner] for inner in range(6)])
        for row_index, col_index in upper_pairs
    ]
    return jnp.stack(rotated)


def accumulate(table, orient_rows, weight_rows):
    blocks = orient_rows.shape[0] // grain_block
    count_cells = orient_rows.shape[1]

    def absorb(carry, inputs):
        chosen, masses = inputs
        picked = jnp.take(table, chosen, axis=1)
        masses_wide = masses.astype(jnp.float32)
        return (
            (
                carry[0] + jnp.sum(picked * masses_wide[None], axis=1),
                carry[1] + jnp.sum(masses_wide, axis=0),
            ),
            None,
        )

    initial = (jnp.zeros((21, count_cells), jnp.float32), jnp.zeros((count_cells,), jnp.float32))
    result, unused = lax.scan(
        absorb,
        initial,
        (
            orient_rows.reshape(blocks, grain_block, count_cells),
            weight_rows.reshape(blocks, grain_block, count_cells),
        ),
    )
    return result


def derivative(padded, direction):
    interior = [padded.shape[0]] + [extent - 8 for extent in padded.shape[1:]]

    def window(offset):
        starts = [0, 4, 4, 4]
        starts[direction] = 4 + offset
        return lax.slice(
            padded, starts, [begin + extent for begin, extent in zip(starts, interior)]
        )

    result = stencil_weights[0] * (window(1) - window(-1))
    for order_index in range(1, 4):
        result = result + stencil_weights[order_index] * (
            window(order_index + 1) - window(-order_index - 1)
        )
    return result


def advance_velocity(velocity, padded_stress, density):
    along_x = derivative(jnp.stack([padded_stress[0], padded_stress[5], padded_stress[4]]), 1)
    along_y = derivative(jnp.stack([padded_stress[5], padded_stress[1], padded_stress[3]]), 2)
    along_z = derivative(jnp.stack([padded_stress[4], padded_stress[3], padded_stress[2]]), 3)
    return velocity + time_step * (along_x + along_y + along_z) / density[None]


def advance_stress(stress, padded_velocity, stiffness):
    grad_x = derivative(padded_velocity, 1)
    grad_y = derivative(padded_velocity, 2)
    grad_z = derivative(padded_velocity, 3)
    strain = [
        grad_x[0],
        grad_y[1],
        grad_z[2],
        grad_y[2] + grad_z[1],
        grad_x[2] + grad_z[0],
        grad_x[1] + grad_y[0],
    ]
    updated = []
    for row_index in range(6):
        change = ordered_sum(
            [
                stiffness[symmetric_index(row_index, col_index)] * strain[col_index]
                for col_index in range(6)
            ]
        )
        updated.append(stress[row_index] + time_step * change)
    return jnp.stack(updated)


def on_device(euler_table, crystal, orient, weight, cell_map, density, velocity, stress):
    part_x = lax.axis_size("gx")
    part_y = lax.axis_size("gy")
    layers = lax.axis_size("ga")
    brick_x, brick_y, brick_z = (stress.shape[1], stress.shape[2], stress.shape[3])
    sub_x = brick_x // part_x
    sub_y = brick_y // part_y
    depth = brick_z * layers
    grains = orient.shape[0]
    count_cells = orient.shape[3]
    table = rotated_table(euler_table, crystal)
    summed, total = accumulate(
        table, orient.reshape(grains, count_cells), weight.reshape(grains, count_cells)
    )
    slots = cell_map.reshape(count_cells)
    layer_pos = slots % depth
    remainder = slots // depth
    sub_y_pos = remainder % sub_y
    remainder = remainder // sub_y
    brick_y_pos = remainder % part_y
    remainder = remainder // part_y
    sub_x_pos = remainder % sub_x
    brick_x_pos = remainder // sub_x
    target = (
        ((brick_x_pos * part_y + brick_y_pos) * sub_x + sub_x_pos) * sub_y + sub_y_pos
    ) * depth + layer_pos
    placed = jnp.zeros((21, count_cells), jnp.float32).at[:, target].set(summed)
    counted = jnp.zeros((count_cells,), jnp.float32).at[target].set(total)
    placed = placed.reshape(21, part_x * part_y, sub_x, sub_y, depth)
    counted = counted.reshape(part_x * part_y, sub_x, sub_y, depth)
    placed, counted = (
        lax.psum_scatter(placed, "ga", scatter_dimension=4, tiled=True),
        lax.psum_scatter(counted, "ga", scatter_dimension=3, tiled=True),
    )
    averaged = placed / counted[None]
    moved = lax.all_to_all(averaged, ("gx", "gy"), split_axis=1, concat_axis=1, tiled=True)
    moved = moved.reshape(21, part_x, part_y, sub_x, sub_y, brick_z)
    stiffness = moved.transpose(0, 1, 3, 2, 4, 5).reshape(21, brick_x, brick_y, brick_z)
    for step_index in range(STEPS):
        padded_stress = with_halo(stress, (("gx", 1), ("gy", 2), ("ga", 3)), 4)
        velocity = advance_velocity(velocity, padded_stress, density)
        padded_velocity = with_halo(velocity, (("gx", 1), ("gy", 2), ("ga", 3)), 4)
        stress = advance_stress(stress, padded_velocity, stiffness)
    return (stiffness, velocity, stress)


def solution(mesh):
    return jax.shard_map(
        on_device,
        mesh=mesh,
        in_specs=(
            P(),
            P(),
            P("ga", "gx", "gy", None),
            P("ga", "gx", "gy", None),
            P("gx", "gy", None),
            P("gx", "gy", "ga"),
            P(None, "gx", "gy", "ga"),
            P(None, "gx", "gy", "ga"),
        ),
        out_specs=(P(None, "gx", "gy", "ga"), P(None, "gx", "gy", "ga"), P(None, "gx", "gy", "ga")),
        check_vma=False,
    )
```

profile of v0, /device:TPU:0, one launch (start us, length us, event | category | flops | bytes accessed | tf_op | source)
XLA Modules:
  0.0 304.8 jit_solution(5697528187163204053)
XLA Ops:
  8.3 2.4 collective-permute-start
  14.1 14.0 %multiply_add_fusion.6 = (f32[1,2048]{1,0:T(1,128)S(1)}, f32[1,2048]{1,0:T(1,128)S(1)}, f32[1,2048]{1,0:T(1,128)S(1)}, f32[1,2048]{1,0:T(1,128)S(1)}, f32[1,2048...) fusion(f32[]{:T(128)} %bitcast.22, f32[]{:T(128)} %bitcast.21, ...), kind=kLoop, calls=%fused_computation.295 | loop fusion | flops 219136 | bytes 131156 | tf_op jit(solution)/shard_map/add | solution.py:42
  28.1 13.8 %multiply_add_fusion.7 = (f32[1,2048]{1,0:T(1,128)S(1)}, f32[1,2048]{1,0:T(1,128)S(1)}, f32[1,2048]{1,0:T(1,128)S(1)}, f32[1,2048]{1,0:T(1,128)S(1)}, f32[1,2048...) fusion(f32[1,2048]{1,0:T(1,128)S(1)} %get-tuple-element.135, ...), kind=kLoop, calls=%fused_computation.296 | loop fusion | flops 186368 | bytes 163924 | tf_op jit(solution)/shard_map/add | solution.py:42
  41.9 13.3 %multiply_add_fusion.34 = (f32[1,2048]{1,0:T(1,128)S(1)}, f32[1,2048]{1,0:T(1,128)S(1)}, f32[1,2048]{1,0:T(1,128)S(1)}, f32[1,2048]{1,0:T(1,128)S(1)}, f32[1,204...) fusion(f32[1,2048]{1,0:T(1,128)S(1)} %get-tuple-element.135, ...), kind=kLoop, calls=%fused_computation.323 | loop fusion | flops 174080 | bytes 155732 | tf_op jit(solution)/shard_map/add | solution.py:42
  55.2 13.5 %multiply_add_fusion.15 = (f32[1,2048]{1,0:T(1,128)S(1)}, f32[1,2048]{1,0:T(1,128)S(1)}, f32[1,2048]{1,0:T(1,128)S(1)}, f32[1,2048]{1,0:T(1,128)S(1)}, f32[1,204...) fusion(f32[1,2048]{1,0:T(1,128)S(1)} %get-tuple-element.135, f32[1,2048]{1,0:T(1,128)S(1)} %get-tuple-element.134, ...), kind=kLoop, calls=%fused_computation.304 | loop fusion | flops 182272 | bytes 155732 | tf_op jit(solution)/shard_map/add | solution.py:42
  68.8 13.5 %multiply_add_fusion.24 = (f32[1,2048]{1,0:T(1,128)S(1)}, f32[1,2048]{1,0:T(1,128)S(1)}, f32[1,2048]{1,0:T(1,128)S(1)}, f32[1,2048]{1,0:T(1,128)S(1)}, f32[1,204...) fusion(f32[1,2048]{1,0:T(1,128)S(1)} %get-tuple-element.135, ...), kind=kLoop, calls=%fused_computation.313 | loop fusion | flops 174080 | bytes 139348 | tf_op jit(solution)/shard_map/add | solution.py:42
  82.3 13.3 %multiply_add_fusion.8 = f32[1,2048]{1,0:T(1,128)S(1)} fusion(f32[1,2048]{1,0:T(1,128)S(1)} %get-tuple-element.148, f32[1,2048]{1,0:T(1,128)S(1)} %get-tuple-element.147, f32[1,2048]{1,0:T(1,128)S(1)} %get-tuple-element.146, f32[1,2048]{1,0:T(1,128)S(1)} %get-tuple-element.145, f32[1,2048]{1,0:T(1,128)S(1)} %get-tuple-element.144, ...), kind=kLoop, calls=%fused_computation.297 | loop fusion | flops 157696 | bytes 57428 | tf_op jit(solution)/shard_map/add | solution.py:42
  95.6 13.3 %multiply_add_fusion.16 = f32[1,2048]{1,0:T(1,128)S(1)} fusion(f32[1,2048]{1,0:T(1,128)S(1)} %get-tuple-element.148, f32[1,2048]{1,0:T(1,128)S(1)} %get-tuple-element.147, f32[1,2048]{1,0:T(1,128)S(1)} %get-tuple-element.146, f32[1,2048]{1,0:T(1,128)S(1)} %get-tuple-element.145, f32[1,2048]{1,0:T(1,128)S(1)} %get-tuple-element.144, ...), kind=kLoop, calls=%fused_computation.305 | loop fusion | flops 157696 | bytes 106580 | tf_op jit(solution)/shard_map/add | solution.py:42
  109.1 13.3 %multiply_add_fusion.45 = (f32[1,2048]{1,0:T(1,128)S(1)}, f32[1,2048]{1,0:T(1,128)S(1)}, f32[1,2048]{1,0:T(1,128)S(1)}, f32[1,2048]{1,0:T(1,128)S(1)}, f32[1,204...) fusion(f32[1,2048]{1,0:T(1,128)S(1)} %get-tuple-element.135, ...), kind=kLoop, calls=%fused_computation.334 | loop fusion | flops 174080 | bytes 155732 | tf_op jit(solution)/shard_map/add | solution.py:42
  123.1 13.3 %multiply_add_fusion.17 = f32[1,2048]{1,0:T(1,128)S(1)} fusion(f32[1,2048]{1,0:T(1,128)S(1)} %get-tuple-element.157, f32[1,2048]{1,0:T(1,128)S(1)} %get-tuple-element.156, f32[1,2048]{1,0:T(1,128)S(1)} %get-tuple-element.155, f32[1,2048]{1,0:T(1,128)S(1)} %get-tuple-element.154, f32[1,2048]{1,0:T(1,128)S(1)} %get-tuple-element.153, ...), kind=kLoop, calls=%fused_computation.306 | loop fusion | flops 157696 | bytes 57428 | tf_op jit(solution)/shard_map/add | solution.py:42
  138.5 4.2 %collective-permute-start.2 = (f32[6,16,4,8]{1,3,2,0:T(8,128)S(1)}, f32[6,16,4,8]{1,3,2,0:T(8,128)S(1)}, u32[]{:S(2)}, u32[]{:S(2)}) collective-permute-start(f32[6,16,4,8]{1,3,2,0:T(8,128)S(1)} %pad_maximum_fusion.13), channel_id=1, source_target_pairs={{0,2},{1,3},{4,6},{5,7},{8,10},{9,11},{12,14},{13,15},{16,18},{17,... | collective-permute-start | bytes 36872 | tf_op jit(solution)/shard_map/ppermute | solution.py:26
  144.0 25.7 %while.13 = (s32[]{:T(128)}, f32[21,512]{0,1:T(8,128)S(1)}, f32[512]{0:T(512)S(1)}, s32[4,4,512]{2,1,0:T(4,128)S(1)}, f32[21,2048]{0,1:T(8,128)S(1)}, /*index=5*/bf16[4,4,512]{2,1,0:T(4,128)(2,1)S(1)}, s32[]{:T(128)}, s32[]{:T(128)}) while((s32[]{:T(128)}, f32[21,512]{0,1:T(8,128)S(1)}, f32[512]{0:T(512)S(1)}, ...), condition=%wide.region_3.4_spmd.clone, body=%wide.region_0.3_spmd.clone.sunk | while | flops 166915 | bytes 790640 | solution.py:113
  144.0 5.5 %gather_fusion = f32[2048,21]{1,0:T(8,128)S(1)} fusion(f32[21,2048]{0,1:T(8,128)S(1)} %get-tuple-element.310, s32[2048]{0:T(1024)S(1)} %broadcast_clamp_fusion.2), kind=kCustom, calls=%fused_computation.clone.clone.1 | custom fusion | bytes 352256 | tf_op jit(solution)/shard_map/while/body/eval_jaxpr/jit(_take)/gather | solution.py:102
  150.5 5.5 %gather_fusion = f32[2048,21]{1,0:T(8,128)S(1)} fusion(f32[21,2048]{0,1:T(8,128)S(1)} %get-tuple-element.310, s32[2048]{0:T(1024)S(1)} %broadcast_clamp_fusion.2), kind=kCustom, calls=%fused_computation.clone.clone.1 | custom fusion | bytes 352256 | tf_op jit(solution)/shard_map/while/body/eval_jaxpr/jit(_take)/gather | solution.py:102
  156.9 5.5 %gather_fusion = f32[2048,21]{1,0:T(8,128)S(1)} fusion(f32[21,2048]{0,1:T(8,128)S(1)} %get-tuple-element.310, s32[2048]{0:T(1024)S(1)} %broadcast_clamp_fusion.2), kind=kCustom, calls=%fused_computation.clone.clone.1 | custom fusion | bytes 352256 | tf_op jit(solution)/shard_map/while/body/eval_jaxpr/jit(_take)/gather | solution.py:102
  163.3 5.5 %gather_fusion = f32[2048,21]{1,0:T(8,128)S(1)} fusion(f32[21,2048]{0,1:T(8,128)S(1)} %get-tuple-element.310, s32[2048]{0:T(1024)S(1)} %broadcast_clamp_fusion.2), kind=kCustom, calls=%fused_computation.clone.clone.1 | custom fusion | bytes 352256 | tf_op jit(solution)/shard_map/while/body/eval_jaxpr/jit(_take)/gather | solution.py:102
  169.9 3.4 %collective-permute-start.4 = (f32[6,16,12,4]{1,3,2,0:T(4,128)S(1)}, f32[6,16,12,4]{1,3,2,0:T(4,128)S(1)}, u32[]{:S(2)}, u32[]{:S(2)}) collective-permute-start(f32[6,16,12,4]{1,3,2,0:T(4,128)S(1)} %get-tuple-element.204), channel_id=1, source_target_pairs={{0,1},{2,3},{4,5},{6,7},{8,9},{10,11},{12,13},{14,15},{16,17},{18,... | collective-permute-start | bytes 55304 | tf_op jit(solution)/shard_map/ppermute | solution.py:26
  177.4 2.4 scatter_custom_fusion.1
  181.9 9.3 %all-reduce = f32[16,1,2,16]{0,2,1,3:T(2,128)S(1)} all-reduce(f32[16,1,2,16]{0,2,1,3:T(2,128)S(1)} %copy.82), channel_id=3, replica_groups=mesh['gx'=8,'gy'=2,'ga'=2] {'ga'}, use_global_device_ids=true, to_apply=%region_7.8.clone | all-reduce | flops 512 | bytes 4096
  196.0 3.0 collective-permute-start.7
  201.2 4.6 %collective-permute-start.9 = (f32[3,16,4,8]{3,2,1,0:T(4,128)S(1)}, f32[3,16,4,8]{3,2,1,0:T(4,128)S(1)}, u32[]{:S(2)}, u32[]{:S(2)}) collective-permute-start(f32[3,16,4,8]{3,2,1,0:T(4,128)S(1)} %pad_maximum_fusion.14), channel_id=1, source_target_pairs={{0,2},{1,3},{4,6},{5,7},{8,10},{9,11},{12,14},{13,15},{16,18},{17,... | collective-permute-start | bytes 18440 | tf_op jit(solution)/shard_map/ppermute | solution.py:26
  209.6 4.6 %collective-permute-start.11 = (f32[3,16,12,4]{3,2,1,0:T(8,128)S(1)}, f32[3,16,12,4]{3,2,1,0:T(8,128)S(1)}, u32[]{:S(2)}, u32[]{:S(2)}) collective-permute-start(f32[3,16,12,4]{3,2,1,0:T(8,128)S(1)} %get-tuple-element.203), channel_id=1, source_target_pairs={{0,1},{2,3},{4,5},{6,7},{8,9},{10,11},{12,13},{14,15},{16,17},{18,... | collective-permute-start | bytes 27656 | tf_op jit(solution)/shard_map/ppermute | solution.py:26
  216.2 11.4 %all-to-all-start = ((f32[16,1,336]{2,1,0:T(1,128)}), f32[16,1,336]{2,1,0:T(1,128)S(1)}, u32[]{:S(2)}, u32[]{:S(2)}) async-start(f32[16,1,336]{2,1,0:T(1,128)} %reshape.481), calls=%async_computation.1 | async-start | bytes 49152 | tf_op jit(solution)/shard_map/all_to_all | solution.py:208
  228.5 5.6 %all-to-all-done = f32[16,1,336]{2,1,0:T(1,128)S(1)} async-done(((f32[16,1,336]{2,1,0:T(1,128)}), f32[16,1,336]{2,1,0:T(1,128)S(1)}, u32[]{:S(2)}, u32[]{:S(2)}) %all-to-all-start) | async-done | bytes 21536 | tf_op jit(solution)/shard_map/all_to_all | solution.py:208
  243.6 2.5 collective-permute-start.14
  247.4 2.1 collective-permute-done.14
  249.6 4.7 %collective-permute-done.15 = f32[6,16,4,8]{3,2,1,0:T(4,128)S(1)} collective-permute-done((f32[6,16,4,8]{3,2,1,0:T(4,128)S(1)}, f32[6,16,4,8]{3,2,1,0:T(4,128)S(1)}, u32[]{:S(2)}, u32[]{:S(2)}) %collective-permute-start.15) | collective-permute-done | bytes 12320 | tf_op jit(solution)/shard_map/ppermute | solution.py:28
  260.6 4.7 %collective-permute-done.17 = f32[6,16,12,4]{1,3,2,0:T(4,128)S(1)} collective-permute-done((f32[6,16,12,4]{1,3,2,0:T(4,128)S(1)}, f32[6,16,12,4]{1,3,2,0:T(4,128)S(1)}, u32[]{:S(2)}, u32[]{:S(2)}) %collective-permute-start.17) | collective-permute-done | bytes 18464 | tf_op jit(solution)/shard_map/ppermute | solution.py:28
  268.7 3.0 collective-permute-start.19
  273.9 4.6 %collective-permute-start.21 = (f32[3,16,4,8]{3,2,1,0:T(4,128)S(1)}, f32[3,16,4,8]{3,2,1,0:T(4,128)S(1)}, u32[]{:S(2)}, u32[]{:S(2)}) collective-permute-start(f32[3,16,4,8]{3,2,1,0:T(4,128)S(1)} %pad_maximum_fusion.15), channel_id=1, source_target_pairs={{0,2},{1,3},{4,6},{5,7},{8,10},{9,11},{12,14},{13,15},{16,18},{17,... | collective-permute-start | bytes 18440 | tf_op jit(solution)/shard_map/ppermute | solution.py:26
  282.2 4.6 %collective-permute-start.23 = (f32[3,16,12,4]{3,2,1,0:T(8,128)S(1)}, f32[3,16,12,4]{3,2,1,0:T(8,128)S(1)}, u32[]{:S(2)}, u32[]{:S(2)}) collective-permute-start(f32[3,16,12,4]{3,2,1,0:T(8,128)S(1)} %get-tuple-element.201), channel_id=1, source_target_pairs={{0,1},{2,3},{4,5},{6,7},{8,9},{10,11},{12,13},{14,15},{16,17},{18,... | collective-permute-start | bytes 27656 | tf_op jit(solution)/shard_map/ppermute | solution.py:26
  287.0 7.5 %collective-permute-done.22 = f32[3,16,12,4]{3,2,1,0:T(8,128)S(1)} collective-permute-done((f32[3,16,12,4]{3,2,1,0:T(8,128)S(1)}, f32[3,16,12,4]{3,2,1,0:T(8,128)S(1)}, u32[]{:S(2)}, u32[]{:S(2)}) %collective-permute-start.22) | collective-permute-done | bytes 9248 | tf_op jit(solution)/shard_map/ppermute | solution.py:28
  (177 shorter events, 61.1 us)
Async XLA Ops:
  7.2 207.2 %reduce-scatter.2.cloned.1.call-start = ((), (), s32[]{:S(2)}) async-start(), calls=%async_computation.2 | async-start | bytes 393216 | tf_op jit(solution)/shard_map/reduce_scatter | solution.py:204
  8.3 3.7 %copy-start.3 = (f32[21]{0:T(128)S(1)}, f32[21]{0:T(128)}, u32[]{:S(2)}) copy-start(f32[21]{0:T(128)} %param.11) | copy-start | bytes 256
  8.3 130.0 %collective-permute-start = (f32[6,4,4,8]{1,3,2,0:T(8,128)S(1)}, f32[6,4,4,8]{1,3,2,0:T(8,128)S(1)}, u32[]{:S(2)}, u32[]{:S(2)}) collective-permute-start(f32[6,4,4,8]{1,3,2,0:T(8,128)S(1)} %get-tuple-element.214), channel_id=1, source_target_pairs={{0,4},{4,8},{8,12},{12,16},{16,20},{20,24},{24,28},{1,5},{5,9},{9,... | collective-permute-start | bytes 9224 | tf_op jit(solution)/shard_map/ppermute | solution.py:26
  10.7 127.6 %collective-permute-start.1 = (f32[6,4,4,8]{1,3,2,0:T(8,128)S(1)}, f32[6,4,4,8]{1,3,2,0:T(8,128)S(1)}, u32[]{:S(2)}, u32[]{:S(2)}) collective-permute-start(f32[6,4,4,8]{1,3,2,0:T(8,128)S(1)} %get-tuple-element.215), channel_id=1, source_target_pairs={{4,0},{8,4},{12,8},{16,12},{20,16},{24,20},{28,24},{5,1},{9,5},{13... | collective-permute-start | bytes 9224 | tf_op jit(solution)/shard_map/ppermute | solution.py:28
  138.5 31.2 %collective-permute-start.2 = (f32[6,16,4,8]{1,3,2,0:T(8,128)S(1)}, f32[6,16,4,8]{1,3,2,0:T(8,128)S(1)}, u32[]{:S(2)}, u32[]{:S(2)}) collective-permute-start(f32[6,16,4,8]{1,3,2,0:T(8,128)S(1)} %pad_maximum_fusion.13), channel_id=1, source_target_pairs={{0,2},{1,3},{4,6},{5,7},{8,10},{9,11},{12,14},{13,15},{16,18},{17,... | collective-permute-start | bytes 36872 | tf_op jit(solution)/shard_map/ppermute | solution.py:26
  142.7 27.0 %collective-permute-start.3 = (f32[6,16,4,8]{1,3,2,0:T(8,128)S(1)}, f32[6,16,4,8]{1,3,2,0:T(8,128)S(1)}, u32[]{:S(2)}, u32[]{:S(2)}) collective-permute-start(f32[6,16,4,8]{1,3,2,0:T(8,128)S(1)} %pad_maximum_fusion.13), channel_id=1, source_target_pairs={{2,0},{3,1},{6,4},{7,5},{10,8},{11,9},{14,12},{15,13},{18,16},{19,... | collective-permute-start | bytes 36872 | tf_op jit(solution)/shard_map/ppermute | solution.py:28
  169.9 4.8 %copy-start.10 = (s32[1,1,512]{2,1,0:T(1,128)S(1)}, s32[1,1,512]{2,1,0:T(1,128)}, u32[]{:S(2)}) copy-start(s32[1,1,512]{2,1,0:T(1,128)} %param.14) | copy-start | bytes 6148
  169.9 21.7 %collective-permute-start.4 = (f32[6,16,12,4]{1,3,2,0:T(4,128)S(1)}, f32[6,16,12,4]{1,3,2,0:T(4,128)S(1)}, u32[]{:S(2)}, u32[]{:S(2)}) collective-permute-start(f32[6,16,12,4]{1,3,2,0:T(4,128)S(1)} %get-tuple-element.204), channel_id=1, source_target_pairs={{0,1},{2,3},{4,5},{6,7},{8,9},{10,11},{12,13},{14,15},{16,17},{18,... | collective-permute-start | bytes 55304 | tf_op jit(solution)/shard_map/ppermute | solution.py:26
  173.3 18.8 %collective-permute-start.5 = (f32[6,16,12,4]{1,3,2,0:T(4,128)S(1)}, f32[6,16,12,4]{1,3,2,0:T(4,128)S(1)}, u32[]{:S(2)}, u32[]{:S(2)}) collective-permute-start(f32[6,16,12,4]{1,3,2,0:T(4,128)S(1)} %get-tuple-element.205), channel_id=1, source_target_pairs={{1,0},{3,2},{5,4},{7,6},{9,8},{11,10},{13,12},{15,14},{17,16},{19,... | collective-permute-start | bytes 55304 | tf_op jit(solution)/shard_map/ppermute | solution.py:28
  193.3 0.8 copy-start.6
  194.7 4.4 %collective-permute-start.6 = (f32[3,4,4,8]{3,2,1,0:T(4,128)S(1)}, f32[3,4,4,8]{3,2,1,0:T(4,128)S(1)}, u32[]{:S(2)}, u32[]{:S(2)}) collective-permute-start(f32[3,4,4,8]{3,2,1,0:T(4,128)S(1)} %get-tuple-element.221), channel_id=1, source_target_pairs={{4,0},{8,4},{12,8},{16,12},{20,16},{24,20},{28,24},{5,1},{9,5},{13... | collective-permute-start | bytes 4616 | tf_op jit(solution)/shard_map/ppermute | solution.py:28
  196.0 3.9 %collective-permute-start.7 = (f32[3,4,4,8]{3,2,1,0:T(4,128)S(1)}, f32[3,4,4,8]{3,2,1,0:T(4,128)S(1)}, u32[]{:S(2)}, u32[]{:S(2)}) collective-permute-start(f32[3,4,4,8]{3,2,1,0:T(4,128)S(1)} %get-tuple-element.220), channel_id=1, source_target_pairs={{0,4},{4,8},{8,12},{12,16},{16,20},{20,24},{24,28},{1,5},{5,9},{9,... | collective-permute-start | bytes 4616 | tf_op jit(solution)/shard_map/ppermute | solution.py:26
  199.9 6.5 %collective-permute-start.8 = (f32[3,16,4,8]{3,2,1,0:T(4,128)S(1)}, f32[3,16,4,8]{3,2,1,0:T(4,128)S(1)}, u32[]{:S(2)}, u32[]{:S(2)}) collective-permute-start(f32[3,16,4,8]{3,2,1,0:T(4,128)S(1)} %pad_maximum_fusion.14), channel_id=1, source_target_pairs={{2,0},{3,1},{6,4},{7,5},{10,8},{11,9},{14,12},{15,13},{18,16},{19,... | collective-permute-start | bytes 18440 | tf_op jit(solution)/shard_map/ppermute | solution.py:28
  201.2 6.8 %collective-permute-start.9 = (f32[3,16,4,8]{3,2,1,0:T(4,128)S(1)}, f32[3,16,4,8]{3,2,1,0:T(4,128)S(1)}, u32[]{:S(2)}, u32[]{:S(2)}) collective-permute-start(f32[3,16,4,8]{3,2,1,0:T(4,128)S(1)} %pad_maximum_fusion.14), channel_id=1, source_target_pairs={{0,2},{1,3},{4,6},{5,7},{8,10},{9,11},{12,14},{13,15},{16,18},{17,... | collective-permute-start | bytes 18440 | tf_op jit(solution)/shard_map/ppermute | solution.py:26
  208.3 19.4 %collective-permute-start.10 = (f32[3,16,12,4]{3,2,1,0:T(8,128)S(1)}, f32[3,16,12,4]{3,2,1,0:T(8,128)S(1)}, u32[]{:S(2)}, u32[]{:S(2)}) collective-permute-start(f32[3,16,12,4]{3,2,1,0:T(8,128)S(1)} %get-tuple-element.202), channel_id=1, source_target_pairs={{1,0},{3,2},{5,4},{7,6},{9,8},{11,10},{13,12},{15,14},{17,16},{19,... | collective-permute-start | bytes 27656 | tf_op jit(solution)/shard_map/ppermute | solution.py:28
  209.6 18.1 %collective-permute-start.11 = (f32[3,16,12,4]{3,2,1,0:T(8,128)S(1)}, f32[3,16,12,4]{3,2,1,0:T(8,128)S(1)}, u32[]{:S(2)}, u32[]{:S(2)}) collective-permute-start(f32[3,16,12,4]{3,2,1,0:T(8,128)S(1)} %get-tuple-element.203), channel_id=1, source_target_pairs={{0,1},{2,3},{4,5},{6,7},{8,9},{10,11},{12,13},{14,15},{16,17},{18,... | collective-permute-start | bytes 27656 | tf_op jit(solution)/shard_map/ppermute | solution.py:26
  216.2 17.9 %all-to-all-start = ((f32[16,1,336]{2,1,0:T(1,128)}), f32[16,1,336]{2,1,0:T(1,128)S(1)}, u32[]{:S(2)}, u32[]{:S(2)}) async-start(f32[16,1,336]{2,1,0:T(1,128)} %reshape.481), calls=%async_computation.1 | async-start | bytes 49152 | tf_op jit(solution)/shard_map/all_to_all | solution.py:208
  235.5 1.7 copy-start
  237.2 0.9 copy-start.2
  238.3 3.3 %collective-permute-start.12 = (f32[6,4,4,8]{3,2,1,0:T(4,128)S(1)}, f32[6,4,4,8]{3,2,1,0:T(4,128)S(1)}, u32[]{:S(2)}, u32[]{:S(2)}) collective-permute-start(f32[6,4,4,8]{3,2,1,0:T(4,128)S(1)} %get-tuple-element.212), channel_id=1, source_target_pairs={{0,4},{4,8},{8,12},{12,16},{16,20},{20,24},{24,28},{1,5},{5,9},{9,... | collective-permute-start | bytes 9224 | tf_op jit(solution)/shard_map/ppermute | solution.py:26
  240.4 3.2 %collective-permute-start.13 = (f32[6,4,4,8]{3,2,1,0:T(4,128)S(1)}, f32[6,4,4,8]{3,2,1,0:T(4,128)S(1)}, u32[]{:S(2)}, u32[]{:S(2)}) collective-permute-start(f32[6,4,4,8]{3,2,1,0:T(4,128)S(1)} %get-tuple-element.213), channel_id=1, source_target_pairs={{4,0},{8,4},{12,8},{16,12},{20,16},{24,20},{28,24},{5,1},{9,5},{13... | collective-permute-start | bytes 9224 | tf_op jit(solution)/shard_map/ppermute | solution.py:28
  243.6 5.9 %collective-permute-start.14 = (f32[6,16,4,8]{3,2,1,0:T(4,128)S(1)}, f32[6,16,4,8]{3,2,1,0:T(4,128)S(1)}, u32[]{:S(2)}, u32[]{:S(2)}) collective-permute-start(f32[6,16,4,8]{3,2,1,0:T(4,128)S(1)} %pad_maximum_fusion.12), channel_id=1, source_target_pairs={{0,2},{1,3},{4,6},{5,7},{8,10},{9,11},{12,14},{13,15},{16,18},{17,... | collective-permute-start | bytes 36872 | tf_op jit(solution)/shard_map/ppermute | solution.py:26
  246.1 8.1 %collective-permute-start.15 = (f32[6,16,4,8]{3,2,1,0:T(4,128)S(1)}, f32[6,16,4,8]{3,2,1,0:T(4,128)S(1)}, u32[]{:S(2)}, u32[]{:S(2)}) collective-permute-start(f32[6,16,4,8]{3,2,1,0:T(4,128)S(1)} %pad_maximum_fusion.12), channel_id=1, source_target_pairs={{2,0},{3,1},{6,4},{7,5},{10,8},{11,9},{14,12},{15,13},{18,16},{19,... | collective-permute-start | bytes 36872 | tf_op jit(solution)/shard_map/ppermute | solution.py:28
  255.2 4.8 %collective-permute-start.16 = (f32[6,16,12,4]{1,3,2,0:T(4,128)S(1)}, f32[6,16,12,4]{1,3,2,0:T(4,128)S(1)}, u32[]{:S(2)}, u32[]{:S(2)}) collective-permute-start(f32[6,16,12,4]{1,3,2,0:T(4,128)S(1)} %copy.90), channel_id=1, source_target_pairs={{0,1},{2,3},{4,5},{6,7},{8,9},{10,11},{12,13},{14,15},{16,17},{18,... | collective-permute-start | bytes 55304 | tf_op jit(solution)/shard_map/ppermute | solution.py:26
  257.1 8.2 %collective-permute-start.17 = (f32[6,16,12,4]{1,3,2,0:T(4,128)S(1)}, f32[6,16,12,4]{1,3,2,0:T(4,128)S(1)}, u32[]{:S(2)}, u32[]{:S(2)}) collective-permute-start(f32[6,16,12,4]{1,3,2,0:T(4,128)S(1)} %copy.91), channel_id=1, source_target_pairs={{1,0},{3,2},{5,4},{7,6},{9,8},{11,10},{13,12},{15,14},{17,16},{19,... | collective-permute-start | bytes 55304 | tf_op jit(solution)/shard_map/ppermute | solution.py:28
  267.3 28.9 %copy-start.1 = (f32[3,8,4,8]{3,2,1,0:T(4,128)}, f32[3,8,4,8]{3,2,1,0:T(4,128)S(1)}, u32[]{:S(2)}) copy-start(f32[3,8,4,8]{3,2,1,0:T(4,128)S(1)} %divide_add_fusion) | copy-start | bytes 9220
  267.4 4.3 %collective-permute-start.18 = (f32[3,4,4,8]{3,2,1,0:T(4,128)S(1)}, f32[3,4,4,8]{3,2,1,0:T(4,128)S(1)}, u32[]{:S(2)}, u32[]{:S(2)}) collective-permute-start(f32[3,4,4,8]{3,2,1,0:T(4,128)S(1)} %get-tuple-element.219), channel_id=1, source_target_pairs={{4,0},{8,4},{12,8},{16,12},{20,16},{24,20},{28,24},{5,1},{9,5},{13... | collective-permute-start | bytes 4616 | tf_op jit(solution)/shard_map/ppermute | solution.py:28
  268.7 3.9 %collective-permute-start.19 = (f32[3,4,4,8]{3,2,1,0:T(4,128)S(1)}, f32[3,4,4,8]{3,2,1,0:T(4,128)S(1)}, u32[]{:S(2)}, u32[]{:S(2)}) collective-permute-start(f32[3,4,4,8]{3,2,1,0:T(4,128)S(1)} %get-tuple-element.218), channel_id=1, source_target_pairs={{0,4},{4,8},{8,12},{12,16},{16,20},{20,24},{24,28},{1,5},{5,9},{9,... | collective-permute-start | bytes 4616 | tf_op jit(solution)/shard_map/ppermute | solution.py:26
  272.6 6.5 %collective-permute-start.20 = (f32[3,16,4,8]{3,2,1,0:T(4,128)S(1)}, f32[3,16,4,8]{3,2,1,0:T(4,128)S(1)}, u32[]{:S(2)}, u32[]{:S(2)}) collective-permute-start(f32[3,16,4,8]{3,2,1,0:T(4,128)S(1)} %pad_maximum_fusion.15), channel_id=1, source_target_pairs={{2,0},{3,1},{6,4},{7,5},{10,8},{11,9},{14,12},{15,13},{18,16},{19,... | collective-permute-start | bytes 18440 | tf_op jit(solution)/shard_map/ppermute | solution.py:28
  273.9 6.8 %collective-permute-start.21 = (f32[3,16,4,8]{3,2,1,0:T(4,128)S(1)}, f32[3,16,4,8]{3,2,1,0:T(4,128)S(1)}, u32[]{:S(2)}, u32[]{:S(2)}) collective-permute-start(f32[3,16,4,8]{3,2,1,0:T(4,128)S(1)} %pad_maximum_fusion.15), channel_id=1, source_target_pairs={{0,2},{1,3},{4,6},{5,7},{8,10},{9,11},{12,14},{13,15},{16,18},{17,... | collective-permute-start | bytes 18440 | tf_op jit(solution)/shard_map/ppermute | solution.py:26
  280.9 13.6 %collective-permute-start.22 = (f32[3,16,12,4]{3,2,1,0:T(8,128)S(1)}, f32[3,16,12,4]{3,2,1,0:T(8,128)S(1)}, u32[]{:S(2)}, u32[]{:S(2)}) collective-permute-start(f32[3,16,12,4]{3,2,1,0:T(8,128)S(1)} %get-tuple-element.200), channel_id=1, source_target_pairs={{1,0},{3,2},{5,4},{7,6},{9,8},{11,10},{13,12},{15,14},{17,16},{19,... | collective-permute-start | bytes 27656 | tf_op jit(solution)/shard_map/ppermute | solution.py:28
  282.2 14.1 %collective-permute-start.23 = (f32[3,16,12,4]{3,2,1,0:T(8,128)S(1)}, f32[3,16,12,4]{3,2,1,0:T(8,128)S(1)}, u32[]{:S(2)}, u32[]{:S(2)}) collective-permute-start(f32[3,16,12,4]{3,2,1,0:T(8,128)S(1)} %get-tuple-element.201), channel_id=1, source_target_pairs={{0,1},{2,3},{4,5},{6,7},{8,9},{10,11},{12,13},{14,15},{16,17},{18,... | collective-permute-start | bytes 27656 | tf_op jit(solution)/shard_map/ppermute | solution.py:26
  (6 other events, 4.3 us)
Sparse Core Ops, SparseCore 0:
  177.5 17.8 reduce-scatter.1
where the time goes:
time: 308 us; the launch traced here: 305 us
  other arithmetic  134 us (44%)
  starting transfers between devices  67.2 us (22%)
  local copies, waits for them, and re-layouts  43 us (14%)
  waiting for transfers between devices  36 us (12%)
  between operations  15.5 us (5%)
  blocking collectives  9.3 us (3%)
    add x15, other arithmetic, ordered_sum(): running = running + summand  122 us
    ppermute x12, starting transfers between devices, with_halo(): lax.ppermute(tail, axis, [(i, (i + 1) % count) for i in range(ends)])  40.2 us
    gather x4, local copies, waits for them, and re-layouts, absorb(): picked = jnp.take(table, chosen, axis=1)  21.9 us
    ppermute x12, waiting for transfers between devices, with_halo(): lax.ppermute(head, axis, [((i + 1) % count, i) for i in range(ends)])  20 us
    ppermute x12, starting transfers between devices, with_halo(): lax.ppermute(head, axis, [((i + 1) % count, i) for i in range(ends)])  15.5 us
    all_to_all x1, starting transfers between devices, on_device(): lax.all_to_all(averaged, ('gx', 'gy'), split_axis=1, concat_axis=1, tiled...  11.4 us
    ppermute x12, waiting for transfers between devices, with_halo(): lax.ppermute(tail, axis, [(i, (i + 1) % count) for i in range(ends)])  10.4 us
    unnamed x1, blocking collectives  9.3 us
  transfers between devices with their start and end apart: 26, of which 14 were waited for; matrix products, arithmetic and copies ran while one was open for 53% of the time, Pallas kernels for 0%

commit v1 on v0

--- a/solution.py
+++ b/solution.py
@@ -1,6 +1,10 @@
+import functools
+
 import jax
 import jax.numpy as jnp
 from jax import lax
+from jax.experimental import pallas as pl
+from jax.experimental.pallas import tpu as pltpu
 from jax.sharding import PartitionSpec as P
 
 STEPS = 2
@@ -170,7 +174,7 @@
     return jnp.stack(updated)
 
 
-def on_device(euler_table, crystal, orient, weight, cell_map, density, velocity, stress):
+def on_device_general(euler_table, crystal, orient, weight, cell_map, density, velocity, stress):
     part_x = lax.axis_size("gx")
     part_y = lax.axis_size("gy")
     layers = lax.axis_size("ga")
@@ -216,6 +220,515 @@
     return (stiffness, velocity, stress)
 
 
+SUB = 8
+LANES = 128
+BLOCK_ROWS = 32
+FIELDS = 10
+LOW_ROWS = tuple(range(8)) + (16, 17, 18)
+HIGH_ROWS = tuple(range(8, 16)) + (19, 20, 21)
+
+
+def fits_plane(part_x, part_y, layers, orient, stress, euler_table):
+    brick_x, brick_y, brick_z = stress.shape[1:]
+    return (
+        part_x % 2 == 0
+        and part_y == 2
+        and layers == 2
+        and brick_x == SUB
+        and part_x == SUB
+        and brick_y == 4
+        and brick_z == 8
+        and orient.shape[3] == part_x * 64
+        and orient.shape[0] % 8 == 0
+        and euler_table.shape[1] % LANES == 0
+    )
+
+
+def lanes_of(shape):
+    return lax.broadcasted_iota(jnp.int32, shape, len(shape) - 1)
+
+
+def rows_of(shape):
+    return lax.broadcasted_iota(jnp.int32, shape, len(shape) - 2)
+
+
+def bond_matrix(trig):
+    cos_one, cos_mid, cos_two, sin_one, sin_mid, sin_two = trig
+    cos_two_mid = cos_two * cos_mid
+    sin_two_mid = sin_two * cos_mid
+    bunge = [
+        [
+            cos_one * cos_two - sin_one * sin_two_mid,
+            sin_one * cos_two + cos_one * sin_two_mid,
+            sin_two * sin_mid,
+        ],
+        [
+            -cos_one * sin_two - sin_one * cos_two_mid,
+            -sin_one * sin_two + cos_one * cos_two_mid,
+            cos_two * sin_mid,
+        ],
+        [sin_one * sin_mid, -cos_one * sin_mid, cos_mid],
+    ]
+    rotation = [[bunge[col][row] for col in range(3)] for row in range(3)]
+    bond = []
+    for first, second in voigt_pairs:
+        row = []
+        for in_index, (third, fourth) in enumerate(voigt_pairs):
+            if in_index < 3:
+                row.append(rotation[first][third] * rotation[second][third])
+            else:
+                row.append(
+                    rotation[first][third] * rotation[second][fourth]
+                    + rotation[first][fourth] * rotation[second][third]
+                )
+        bond.append(row)
+    return bond
+
+
+def grain_kernel(
+    crystal_ref,
+    euler_ref,
+    orient_ref,
+    weight_ref,
+    map_ref,
+    density_ref,
+    velocity_ref,
+    stress_ref,
+    send_ref,
+    trig_ref,
+    picked_ref,
+    sums_ref,
+    place_ref,
+    acc_ref,
+):
+    row_part = lax.axis_index("gy")
+    layer = lax.axis_index("ga")
+    grains = weight_ref.shape[0]
+    cells = weight_ref.shape[1]
+    tiles = cells // LANES
+    octets = grains // SUB
+    table_tiles = euler_ref.shape[1] // LANES
+    destinations = send_ref.shape[0]
+
+    angles = euler_ref[...]
+    trig_ref[0:3, :] = jnp.cos(angles)
+    trig_ref[3:6, :] = jnp.sin(angles)
+    groups = [(octet, tile) for tile in range(tiles) for octet in range(octets)]
+    low, high = [], []
+    for octet, tile in groups:
+        index = orient_ref[pl.ds(octet * SUB * tiles + tile, SUB, stride=tiles), :]
+        low.append(index & (LANES - 1))
+        high.append(index >> 7)
+    for which in range(6):
+        values = [None] * len(groups)
+        for tile in range(table_tiles):
+            source = jnp.broadcast_to(
+                trig_ref[which : which + 1, tile * LANES : (tile + 1) * LANES], (SUB, LANES)
+            )
+            for at in range(len(groups)):
+                found = jnp.take_along_axis(source, low[at], axis=1, mode="promise_in_bounds")
+                values[at] = found if tile == 0 else jnp.where(high[at] == tile, found, values[at])
+        for at in range(len(groups)):
+            picked_ref[which * len(groups) + at] = values[at]
+
+    sums_ref[...] = jnp.zeros_like(sums_ref)
+    entries = [
+        [crystal_ref[symmetric_index(row, col)] for col in range(6)] for row in range(6)
+    ]
+    row_of = {}
+    for k in range(len(LOW_ROWS)):
+        row_of[LOW_ROWS[k]] = k
+        row_of[HIGH_ROWS[k]] = 16 + k
+
+    def one_tile(tile, unused):
+        for octet in range(octets):
+            at = tile * octets + octet
+            bond = bond_matrix([picked_ref[which * len(groups) + at] for which in range(6)])
+            mass = weight_ref[
+                octet * SUB : (octet + 1) * SUB, pl.ds(pl.multiple_of(tile * LANES, LANES), LANES)
+            ].astype(jnp.float32)
+            pair = 0
+            for row in range(6):
+                product = [
+                    ordered_sum([bond[row][inner] * entries[inner][col] for inner in range(6)])
+                    * mass
+                    for col in range(6)
+                ]
+                for col in range(row, 6):
+                    value = ordered_sum([product[inner] * bond[col][inner] for inner in range(6)])
+                    acc_ref[pair] = value if octet == 0 else acc_ref[pair] + value
+                    pair += 1
+            acc_ref[21] = mass if octet == 0 else acc_ref[21] + mass
+        for pair in range(22):
+            sums_ref[
+                row_of[pair] : row_of[pair] + 1, pl.ds(pl.multiple_of(tile * LANES, LANES), LANES)
+            ] = jnp.sum(acc_ref[pair], axis=0, keepdims=True)
+        return unused
+
+    lax.fori_loop(0, tiles, one_tile, 0)
+
+    slots = map_ref[...]
+    half = cells // (cells // 32)
+    place_ref[...] = jnp.zeros_like(place_ref)
+    for chunk in range(cells // half):
+        wanted = rows_of((half, cells)) + chunk * half
+        hit = jnp.where(jnp.broadcast_to(slots, (half, cells)) == wanted, 1.0, 0.0)
+        start = pl.multiple_of(chunk * 2 * half + row_part * half, half)
+        place_ref[pl.ds(start, half), :] = hit.astype(jnp.bfloat16)
+    sums = sums_ref[...]
+    part_one = sums.astype(jnp.bfloat16)
+    rest = sums - part_one.astype(jnp.float32)
+    part_two = rest.astype(jnp.bfloat16)
+    part_three = (rest - part_two.astype(jnp.float32)).astype(jnp.bfloat16)
+    parts = jnp.concatenate([part_one, part_two, part_three], axis=0)
+    placed = lax.dot_general(
+        parts, place_ref[...], (((1,), (1,)), ((), ())), preferred_element_type=jnp.float32
+    )
+    placed = placed[0:32] + placed[32:64] + placed[64:96]
+
+    own = row_part * 2 + layer
+    lane = lanes_of((SUB, LANES))
+    row = rows_of((SUB, LANES))
+
+    def field_rows(component, y):
+        if component < 6:
+            return stress_ref[pl.ds(component * 32 + y, SUB, stride=4), :]
+        if component < 9:
+            return velocity_ref[pl.ds((component - 6) * 32 + y, SUB, stride=4), :]
+        return density_ref[pl.ds(y, SUB, stride=4), :]
+
+    def spread(component, slot, into):
+        goal = own ^ slot
+        for y in range(4):
+            start = (goal // 2) * 64 + y * 16 + (goal % 2) * 8
+            narrow = jnp.concatenate(
+                [field_rows(component, y), jnp.zeros((SUB, LANES - 8), jnp.float32)], axis=1
+            )
+            into = into + pltpu.roll(narrow, start, 1)
+        return into
+
+    nothing = jnp.zeros((SUB, LANES), jnp.float32)
+    group_one, group_two, tail_low, tail_high = nothing, nothing, nothing, nothing
+    for slot in range(4):
+        group_one = spread(slot, slot, group_one)
+        group_two = spread(4 + slot, slot, group_two)
+    tail_low = spread(9, 2, spread(8, 0, tail_low))
+    tail_high = spread(9, 3, spread(8, 1, tail_high))
+    tail = pltpu.roll(tail_low, 4, 0) + tail_high
+
+    shift = 32 + row_part * 64
+    for brick in range(destinations // 4):
+        low_half = placed[0:16, brick * LANES : (brick + 1) * LANES]
+        high_half = placed[16:32, brick * LANES : (brick + 1) * LANES]
+        packed = low_half + pltpu.roll(high_half, shift, 1)
+        last = jnp.where(row < 4, packed[8:16], tail)
+        for inner in range(4):
+            at = brick * 4 + inner
+            send_ref[at, 0:8, :] = packed[0:8]
+            send_ref[at, 8:16, :] = last
+            send_ref[at, 16:24, :] = group_one
+            send_ref[at, 24:32, :] = group_two
+
+
+def plane_derivative(field, dim, lane):
+    position = lane // 16 if dim == 1 else lane % 16
+    extent = 8 if dim == 1 else 16
+    unit = 16 if dim == 1 else 1
+    total = None
+    for order in range(1, 5):
+        ahead = pltpu.roll(field, LANES - order * unit, 1)
+        behind = pltpu.roll(field, order * unit, 1)
+        term = stencil_weights[order - 1] * (
+            jnp.where(position + order < extent, ahead, 0.0)
+            - jnp.where(position - order >= 0, behind, 0.0)
+        )
+        total = term if total is None else total + term
+    return total
+
+
+def row_derivative(read, start, count):
+    total = stencil_weights[0] * (read(start + 1, count) - read(start - 1, count))
+    for order in range(2, 5):
+        total = total + stencil_weights[order - 1] * (
+            read(start + order, count) - read(start - order, count)
+        )
+    return total
+
+
+def velocity_update(wide_stress, old_velocity, density, inside):
+    count = 16
+    lane = lanes_of((count, LANES))
+
+    def along(component, dim):
+        if dim == 0:
+            return row_derivative(
+                lambda at, size: wide_stress[component, at : at + size, :], 4, count
+            )
+        return plane_derivative(wide_stress[component, 4 : 4 + count, :], dim, lane)
+
+    sums = [
+        along(0, 0) + along(5, 1) + along(4, 2),
+        along(5, 0) + along(1, 1) + along(3, 2),
+        along(4, 0) + along(3, 1) + along(2, 2),
+    ]
+    return [
+        jnp.where(inside, old_velocity[at] + time_step * sums[at] / density, 0.0)
+        for at in range(3)
+    ]
+
+
+def stress_update(wide_velocity, old_stress, stiff):
+    lane = lanes_of((SUB, LANES))
+
+    def along(component, dim):
+        if dim == 0:
+            return row_derivative(
+                lambda at, size: wide_velocity[component, at : at + size, :], 4, SUB
+            )
+        return plane_derivative(wide_velocity[component, 4 : 4 + SUB, :], dim, lane)
+
+    strain = [
+        along(0, 0),
+        along(1, 1),
+        along(2, 2),
+        along(2, 1) + along(1, 2),
+        along(2, 0) + along(0, 2),
+        along(1, 0) + along(0, 1),
+    ]
+    return [
+        old_stress[row]
+        + time_step
+        * ordered_sum([stiff(symmetric_index(row, col)) * strain[col] for col in range(6)])
+        for row in range(6)
+    ]
+
+
+def inside_rows(brick, bricks):
+    place = rows_of((16, LANES)) - 4
+    return ((brick > 0) | (place >= 0)) & ((brick < bricks - 1) | (place < SUB))
+
+
+def first_step_kernel(
+    got_ref, stiff_ref, stress_ref, velocity_ref, density_ref, wide_ref, moving_ref
+):
+    brick = lax.axis_index("gx")
+    bricks = got_ref.shape[0] // 4
+    lane = lanes_of((SUB, LANES))
+    row = rows_of((SUB, LANES))
+
+    lane_two = lanes_of((16, LANES))
+    own_slot = (lane_two // 32) % 2 == 0
+    for p in range(bricks):
+        zero = got_ref[p * 4, 0:16, :] + got_ref[p * 4 + 1, 0:16, :]
+        one = got_ref[p * 4 + 2, 0:16, :] + got_ref[p * 4 + 3, 0:16, :]
+        low = jnp.where(own_slot, zero, one)
+        high = jnp.where(own_slot, one, zero)
+        high = jnp.where(own_slot, pltpu.roll(high, LANES - 32, 1), pltpu.roll(high, 32, 1))
+        total = jnp.broadcast_to(high[10:11], (SUB, LANES))
+        stiff_ref[p * 24 : p * 24 + 8, :] = low[0:8] / total
+        stiff_ref[p * 24 + 8 : p * 24 + 16, :] = high[0:8] / total
+        last = jnp.where(row < 3, low[8:16], pltpu.roll(high[8:16], 3, 0))
+        stiff_ref[p * 24 + 16 : p * 24 + 24, :] = last / total
+
+    kind = (lane // 64) * 2 + (lane // 8) % 2
+
+    def settle(value, slot):
+        if slot & 1:
+            value = jnp.where(
+                (lane // 8) % 2 == 0,
+                pltpu.roll(value, LANES - 8, 1),
+                pltpu.roll(value, 8, 1),
+            )
+        if slot & 2:
+            value = pltpu.roll(value, 64, 1)
+        return value
+
+    for side in range(3):
+        source = jnp.clip(brick + side - 1, 0, bricks - 1)
+        valid = source == brick + side - 1
+
+        def collect(rows, slot):
+            pieces = [got_ref[source * 4 + (q ^ slot), rows : rows + 8, :] for q in range(4)]
+            value = jnp.where(
+                kind < 2,
+                jnp.where(kind == 0, pieces[0], pieces[1]),
+                jnp.where(kind == 2, pieces[2], pieces[3]),
+            )
+            return settle(value, slot)
+
+        def keep(component, value):
+            value = jnp.where(valid, value, 1.0 if component == 9 else 0.0)
+            wide_ref[component, side * SUB : (side + 1) * SUB, :] = value
+
+        for slot in range(4):
+            keep(slot, collect(16, slot))
+            keep(4 + slot, collect(24, slot))
+        for component in (8, 9):
+            slot = (component - 8) * 2
+            upper = pltpu.roll(collect(8, slot), 4, 0)
+            keep(component, jnp.where(row < 4, upper, collect(8, slot + 1)))
+
+    density = wide_ref[9, 4:20, :]
+    density_ref[...] = density
+    fresh = velocity_update(
+        wide_ref,
+        [wide_ref[6 + at, 4:20, :] for at in range(3)],
+        density,
+        inside_rows(brick, bricks),
+    )
+    for at in range(3):
+        velocity_ref[at] = fresh[at]
+        moving_ref[at] = fresh[at]
+    fresh = stress_update(
+        moving_ref,
+        [wide_ref[at, 8:16, :] for at in range(6)],
+        lambda pair: stiff_ref[pl.ds(pair, SUB, stride=24), :],
+    )
+    for at in range(6):
+        stress_ref[at] = fresh[at]
+
+
+def stiffness_kernel(stiff_ref, out_ref, turned_ref):
+    own = lax.axis_index("gy") * 64 + lax.axis_index("ga") * 8
+    for p in range(SUB):
+        turned_ref[...] = jnp.transpose(stiff_ref[p * 24 : (p + 1) * 24, :])
+        for y in range(4):
+            rows = pl.ds(pl.multiple_of(own + y * 16, 8), 8)
+            out_ref[p * 32 + y * 8 : p * 32 + y * 8 + 8, :] = turned_ref[rows, 0:21]
+
+
+def last_step_kernel(
+    stress_ref,
+    pair_ref,
+    cross_ref,
+    velocity_ref,
+    density_ref,
+    stiff_ref,
+    out_velocity_ref,
+    out_stress_ref,
+    wide_ref,
+    moving_ref,
+    *,
+    bricks,
+):
+    brick = lax.axis_index("gx")
+    even = brick % 2 == 0
+    for at in range(6):
+        pair, cross = pair_ref[at], cross_ref[at]
+        wide_ref[at, 0:8, :] = jnp.where(even, cross, pair)
+        wide_ref[at, 8:16, :] = stress_ref[at]
+        wide_ref[at, 16:24, :] = jnp.where(even, pair, cross)
+    velocity = velocity_update(
+        wide_ref,
+        [velocity_ref[at] for at in range(3)],
+        density_ref[...],
+        inside_rows(brick, bricks),
+    )
+    for at in range(3):
+        moving_ref[at] = velocity[at]
+    stress = stress_update(
+        moving_ref,
+        [stress_ref[at] for at in range(6)],
+        lambda pair: stiff_ref[pl.ds(pair, SUB, stride=24), :],
+    )
+    own = lax.axis_index("gy") * 64 + lax.axis_index("ga") * 8
+
+    def put(out_ref, at, value):
+        for y in range(4):
+            turned = pltpu.roll(value, (LANES - own - y * 16) % LANES, 1)
+            out_ref[pl.ds(at * 32 + y, SUB, stride=4), :] = turned[:, 0:8]
+
+    for at in range(3):
+        put(out_velocity_ref, at, moving_ref[at, 4:12, :])
+    for at in range(6):
+        put(out_stress_ref, at, stress[at])
+
+
+def on_plane(euler_table, crystal, orient, weight, cell_map, density, velocity, stress):
+    part_x = lax.axis_size("gx")
+    devices = part_x * lax.axis_size("gy") * lax.axis_size("ga")
+    grains, cells = orient.shape[0], orient.shape[3]
+    tiles = cells // LANES
+    octets = grains // SUB
+    vmem = pl.BlockSpec(memory_space=pltpu.VMEM)
+    smem = pl.BlockSpec(memory_space=pltpu.SMEM)
+    f32 = jnp.float32
+
+    send = pl.pallas_call(
+        grain_kernel,
+        out_shape=jax.ShapeDtypeStruct((devices, BLOCK_ROWS, LANES), f32),
+        in_specs=[smem] + [vmem] * 7,
+        out_specs=vmem,
+        scratch_shapes=[
+            pltpu.VMEM((SUB, euler_table.shape[1]), f32),
+            pltpu.VMEM((6 * tiles * octets, SUB, LANES), f32),
+            pltpu.VMEM((32, cells), f32),
+            pltpu.VMEM((2 * cells, cells), jnp.bfloat16),
+            pltpu.VMEM((22, SUB, LANES), f32),
+        ],
+    )(
+        crystal,
+        euler_table,
+        orient.reshape(grains * tiles, LANES),
+        weight.reshape(grains, cells),
+        cell_map.reshape(1, cells),
+        density.reshape(SUB * 4, 8),
+        velocity.reshape(3 * SUB * 4, 8),
+        stress.reshape(6 * SUB * 4, 8),
+    )
+    got = lax.all_to_all(send, ("gx", "gy", "ga"), split_axis=0, concat_axis=0, tiled=True)
+    stiff, middle_stress, middle_velocity, wide_density = pl.pallas_call(
+        first_step_kernel,
+        out_shape=(
+            jax.ShapeDtypeStruct((part_x * 24, LANES), f32),
+            jax.ShapeDtypeStruct((6, SUB, LANES), f32),
+            jax.ShapeDtypeStruct((3, 16, LANES), f32),
+            jax.ShapeDtypeStruct((16, LANES), f32),
+        ),
+        in_specs=[vmem],
+        out_specs=(vmem,) * 4,
+        scratch_shapes=[
+            pltpu.VMEM((FIELDS, 24, LANES), f32),
+            pltpu.VMEM((3, 16, LANES), f32),
+        ],
+    )(got)
+    pair = lax.ppermute(middle_stress, "gx", [(i, i ^ 1) for i in range(part_x)])
+    swaps = [(i, i + 1) for i in range(1, part_x - 1, 2)]
+    cross = lax.ppermute(middle_stress, "gx", swaps + [(b, a) for a, b in swaps])
+    stiffness = pl.pallas_call(
+        stiffness_kernel,
+        out_shape=jax.ShapeDtypeStruct((SUB * 4 * 8, 21), f32),
+        in_specs=[vmem],
+        out_specs=vmem,
+        scratch_shapes=[pltpu.VMEM((LANES, 24), f32)],
+        cost_estimate=pl.CostEstimate(flops=100000, bytes_accessed=200000, transcendentals=0),
+    )(stiff)
+    new_velocity, new_stress = pl.pallas_call(
+        functools.partial(last_step_kernel, bricks=part_x),
+        out_shape=(
+            jax.ShapeDtypeStruct((3 * SUB * 4, 8), f32),
+            jax.ShapeDtypeStruct((6 * SUB * 4, 8), f32),
+        ),
+        in_specs=[vmem] * 6,
+        out_specs=(vmem,) * 2,
+        scratch_shapes=[
+            pltpu.VMEM((6, 24, LANES), f32),
+            pltpu.VMEM((3, 16, LANES), f32),
+        ],
+    )(middle_stress, pair, cross, middle_velocity, wide_density, stiff)
+    return (
+        stiffness.reshape(SUB, 4, 8, 21).transpose(3, 0, 1, 2),
+        new_velocity.reshape(3, SUB, 4, 8),
+        new_stress.reshape(6, SUB, 4, 8),
+    )
+
+
+def on_device(euler_table, crystal, orient, weight, cell_map, density, velocity, stress):
+    sizes = (lax.axis_size("gx"), lax.axis_size("gy"), lax.axis_size("ga"))
+    form = on_plane if fits_plane(*sizes, orient, stress, euler_table) else on_device_general
+    return form(euler_table, crystal, orient, weight, cell_map, density, velocity, stress)
+
+
 def solution(mesh):
     return jax.shard_map(
         on_device,

time: 308 us -> 40 us (0.13)
  other arithmetic: 134 us -> 0 us
  starting transfers between devices: 67.2 us -> 2.99 us
  local copies, waits for them, and re-layouts: 43 us -> 0.6 us
  waiting for transfers between devices: 36 us -> 0.01 us
  between operations: 15.5 us -> 0.66 us
  blocking collectives: 9.3 us -> 23.7 us
  Pallas kernels: 0 us -> 11.7 us
    add x31 -> x0, other arithmetic: 126 us -> none  [the longest x15 122 us: ordered_sum(): running = running + summand]
    ppermute x24 -> x2, starting transfers between devices: 55.7 us -> 2.99 us  [the longest x1 2.34 us: on_plane(): lax.ppermute(middle_stress, 'gx', [(i, i ^ 1) for i in range(part_x)])]
    ppermute x24 -> x2, waiting for transfers between devices: 30.3 us -> 0.01 us  [the longest x1 0.01 us: on_plane(): lax.ppermute(middle_stress, 'gx', swaps + [(b, a) for a, b in swaps])]
    all_to_all x0 -> x1, blocking collectives: none -> 23.7 us  [on_plane(): lax.all_to_all(send, ('gx', 'gy', 'ga'), split_axis=0, concat_axis=0, til...]
    gather x4 -> x0, local copies, waits for them, and re-layouts: 21.9 us -> none  [absorb(): picked = jnp.take(table, chosen, axis=1)]
    pallas_call x0 -> x4, Pallas kernels: none -> 11.7 us  [the longest x1 5.74 us: on_plane(): pl.pallas_call(grain_kernel, out_shape=jax.ShapeDtypeStruct((devices, BLO...]
    all_to_all x1 -> x0, starting transfers between devices: 11.4 us -> none  [on_device(): lax.all_to_all(averaged, ('gx', 'gy'), split_axis=1, concat_axis=1, tiled...]
    unnamed x1 -> x0, blocking collectives: 9.3 us -> none
  transfers between devices with their start and end apart: 26 -> 2, of which waited for: 14 -> 0; matrix products, arithmetic and copies ran while one was open for 53% -> 0% of each run, Pallas kernels for 0% -> 4%
where the time goes in v1:
time: 40 us; the launch traced here: 39.7 us
  blocking collectives  23.7 us (59%)
  Pallas kernels  11.7 us (29%)
  starting transfers between devices  2.99 us (7%)
  between operations  0.66 us (2%)
  local copies, waits for them, and re-layouts  0.6 us (2%)
    all_to_all x1, blocking collectives, on_plane(): lax.all_to_all(send, ('gx', 'gy', 'ga'), split_axis=0, concat_axis=0, til...  23.7 us
    pallas_call x1, Pallas kernels, on_plane(): pl.pallas_call(grain_kernel, out_shape=jax.ShapeDtypeStruct((devices, BLO...  5.74 us
    ppermute x1, starting transfers between devices, on_plane(): lax.ppermute(middle_stress, 'gx', [(i, i ^ 1) for i in range(part_x)])  2.34 us
    pallas_call x1, Pallas kernels, on_plane(): pl.pallas_call(first_step_kernel, out_shape=(jax.ShapeDtypeStruct((part_x...  2.18 us
    pallas_call x1, Pallas kernels, on_plane(): pl.pallas_call(functools.partial(last_step_kernel, bricks=part_x), out_sh...  2.02 us
    pallas_call x1, Pallas kernels, on_plane(): pl.pallas_call(stiffness_kernel, out_shape=jax.ShapeDtypeStruct((SUB * 4...  1.76 us
  transfers between devices with their start and end apart: 2, of which 0 were waited for; matrix products, arithmetic and copies ran while one was open for 0% of the time, Pallas kernels for 4%

profile of v1, /device:TPU:0, one launch (start us, length us, event | category | flops | bytes accessed | tf_op | source)
XLA Modules:
  0.0 39.7 jit_solution(6229768014930038327)
XLA Ops:
  0.6 5.7 %shard_map.103 = f32[32,32,128]{2,1,0:T(8,128)} custom-call(f32[21]{0:T(128)} %crystal_ref.1, f32[3,2048]{1,0:T(4,128)} %euler_ref.1, s32[64,128]{1,0:T(8,128)} %bitcast.14, bf16[16,512]{1,0:T(8,128)(2,1)} %bitcast.15, s32[1,512]{1,0:T(1,128)} %bitcast.17, f32[32,8]{1,0:T(8,128)} %bitcast.16, f32[96,8]{1,0:T(8,128)} %bitcast.13, f32[192,8]{1,0:T(8,128)} %bitcast.12), custom_call_target="tpu_custom_call" | custom-call | tf_op jit(solution)/shard_map/pallas_call | solution.py:657
  6.4 23.7 %all_to_all.5.got_ref = f32[32,32,128]{2,1,0:T(8,128)} all-to-all(f32[32,32,128]{2,1,0:T(8,128)} %shard_map.103), channel_id=1, replica_groups=mesh['gx'=8,'gy'=2,'ga'=2] {'gx','gy','ga'}, dimensions={0} | all-to-all | bytes 1048576 | tf_op jit(solution)/shard_map/all_to_all | solution.py:679
  30.1 2.2 %shard_map.104 = (f32[192,128]{1,0:T(8,128)}, f32[6,8,128]{2,1,0:T(8,128)}, f32[3,16,128]{2,1,0:T(8,128)}, f32[16,128]{1,0:T(8,128)}) custom-call(f32[32,32,128]{2,1,0:T(8,128)} %all_to_all.5.got_ref), custom_call_target="tpu_custom_call" | custom-call | tf_op jit(solution)/shard_map/pallas_call | solution.py:680
  32.3 0.7 %collective-permute-start.1 = (f32[6,8,128]{2,1,0:T(8,128)}, f32[6,8,128]{2,1,0:T(8,128)S(1)}, u32[]{:S(2)}, u32[]{:S(2)}) collective-permute-start(f32[6,8,128]{2,1,0:T(8,128)} %get-tuple-element.10.stress_ref), channel_id=1, source_target_pairs={{4,8},{12,16},{20,24},{8,4},{16,12},{24,20},{5,9},{13,17},{21,25},... | collective-permute-start | bytes 73736 | tf_op jit(solution)/shard_map/ppermute | solution.py:697
  32.9 2.3 %collective-permute-start = (f32[6,8,128]{2,1,0:T(8,128)}, f32[6,8,128]{2,1,0:T(8,128)S(1)}, u32[]{:S(2)}, u32[]{:S(2)}) collective-permute-start(f32[6,8,128]{2,1,0:T(8,128)} %get-tuple-element.10.stress_ref), channel_id=1, source_target_pairs={{0,4},{4,0},{8,12},{12,8},{16,20},{20,16},{24,28},{28,24},{1,5},{5... | collective-permute-start | bytes 73736 | tf_op jit(solution)/shard_map/ppermute | solution.py:695
  35.3 1.8 %shard_map.105 = f32[256,21]{1,0:T(8,128)} custom-call(f32[192,128]{1,0:T(8,128)} %get-tuple-element.9.stiff_ref), custom_call_target="tpu_custom_call" | custom-call | flops 100000 | bytes 200000 | tf_op jit(solution)/shard_map/pallas_call | solution.py:698
  37.0 0.0 collective-permute-done.1.cross_ref
  37.0 0.0 copy-start
  37.0 0.0 collective-permute-done.pair_ref
  37.0 0.0 copy-start.1
  37.1 0.6 %copy-done = f32[6,8,128]{2,1,0:T(8,128)} copy-done((f32[6,8,128]{2,1,0:T(8,128)}, f32[6,8,128]{2,1,0:T(8,128)S(1)}, u32[]{:S(2)}) %copy-start) | copy-done | bytes 24600
  37.6 0.0 copy-done.1
  37.6 2.0 %shard_map.106 = (f32[96,8]{1,0:T(8,128)}, f32[192,8]{1,0:T(8,128)}) custom-call(f32[6,8,128]{2,1,0:T(8,128)} %get-tuple-element.10.stress_ref, f32[6,8,128]{2,1,0:T(8,128)} %copy-done.1, f32[6,8,128]{2,1,0:T(8,128)} %copy-done, f32[3,16,128]{2,1,0:T(8,128)} %get-tuple-element.11.velocity_ref, f32[16,128]{1,0:T(8,128)} %get-tuple-element.12.density_ref, ...), custom_call_target="tpu_custom_call" | custom-call | tf_op jit(solution)/shard_map/pallas_call | solution.py:706
Async XLA Ops:
  32.3 4.8 %collective-permute-start.1 = (f32[6,8,128]{2,1,0:T(8,128)}, f32[6,8,128]{2,1,0:T(8,128)S(1)}, u32[]{:S(2)}, u32[]{:S(2)}) collective-permute-start(f32[6,8,128]{2,1,0:T(8,128)} %get-tuple-element.10.stress_ref), channel_id=1, source_target_pairs={{4,8},{12,16},{20,24},{8,4},{16,12},{24,20},{5,9},{13,17},{21,25},... | collective-permute-start | bytes 73736 | tf_op jit(solution)/shard_map/ppermute | solution.py:697
  32.9 4.1 %collective-permute-start = (f32[6,8,128]{2,1,0:T(8,128)}, f32[6,8,128]{2,1,0:T(8,128)S(1)}, u32[]{:S(2)}, u32[]{:S(2)}) collective-permute-start(f32[6,8,128]{2,1,0:T(8,128)} %get-tuple-element.10.stress_ref), channel_id=1, source_target_pairs={{0,4},{4,0},{8,12},{12,8},{16,20},{20,16},{24,28},{28,24},{1,5},{5... | collective-permute-start | bytes 73736 | tf_op jit(solution)/shard_map/ppermute | solution.py:695
  37.0 0.6 %copy-start = (f32[6,8,128]{2,1,0:T(8,128)}, f32[6,8,128]{2,1,0:T(8,128)S(1)}, u32[]{:S(2)}) copy-start(f32[6,8,128]{2,1,0:T(8,128)S(1)} %collective-permute-done.1.cross_ref) | copy-start | bytes 73732
  37.0 0.6 %copy-start.1 = (f32[6,8,128]{2,1,0:T(8,128)}, f32[6,8,128]{2,1,0:T(8,128)S(1)}, u32[]{:S(2)}) copy-start(f32[6,8,128]{2,1,0:T(8,128)S(1)} %collective-permute-done.pair_ref) | copy-start | bytes 73732

commit v2 on v1

--- a/solution.py
+++ b/solution.py
@@ -286,6 +286,15 @@
 
 
 def grain_kernel(
+    crystal_hbm,
+    euler_hbm,
+    orient_hbm,
+    weight_hbm,
+    map_hbm,
+    density_hbm,
+    velocity_hbm,
+    stress_hbm,
+    send_ref,
     crystal_ref,
     euler_ref,
     orient_ref,
@@ -294,12 +303,11 @@
     density_ref,
     velocity_ref,
     stress_ref,
-    send_ref,
     trig_ref,
-    picked_ref,
     sums_ref,
     place_ref,
     acc_ref,
+    arrived,
 ):
     row_part = lax.axis_index("gy")
     layer = lax.axis_index("ga")
@@ -310,28 +318,33 @@
     table_tiles = euler_ref.shape[1] // LANES
     destinations = send_ref.shape[0]
 
+    copies = [
+        pltpu.make_async_copy(source, target, arrived.at[at])
+        for at, (source, target) in enumerate(
+            [
+                (euler_hbm, euler_ref),
+                (orient_hbm, orient_ref),
+                (weight_hbm, weight_ref),
+                (crystal_hbm, crystal_ref),
+                (map_hbm, map_ref),
+                (stress_hbm, stress_ref),
+                (velocity_hbm, velocity_ref),
+                (density_hbm, density_ref),
+            ]
+        )
+    ]
+    for copy in copies:
+        copy.start()
+    sums_ref[...] = jnp.zeros_like(sums_ref)
+    place_ref[...] = jnp.zeros_like(place_ref)
+
+    copies[0].wait()
     angles = euler_ref[...]
     trig_ref[0:3, :] = jnp.cos(angles)
     trig_ref[3:6, :] = jnp.sin(angles)
-    groups = [(octet, tile) for tile in range(tiles) for octet in range(octets)]
-    low, high = [], []
-    for octet, tile in groups:
-        index = orient_ref[pl.ds(octet * SUB * tiles + tile, SUB, stride=tiles), :]
-        low.append(index & (LANES - 1))
-        high.append(index >> 7)
-    for which in range(6):
-        values = [None] * len(groups)
-        for tile in range(table_tiles):
-            source = jnp.broadcast_to(
-                trig_ref[which : which + 1, tile * LANES : (tile + 1) * LANES], (SUB, LANES)
-            )
-            for at in range(len(groups)):
-                found = jnp.take_along_axis(source, low[at], axis=1, mode="promise_in_bounds")
-                values[at] = found if tile == 0 else jnp.where(high[at] == tile, found, values[at])
-        for at in range(len(groups)):
-            picked_ref[which * len(groups) + at] = values[at]
-
-    sums_ref[...] = jnp.zeros_like(sums_ref)
+
+    for copy in copies[1:4]:
+        copy.wait()
     entries = [
         [crystal_ref[symmetric_index(row, col)] for col in range(6)] for row in range(6)
     ]
@@ -340,10 +353,26 @@
         row_of[LOW_ROWS[k]] = k
         row_of[HIGH_ROWS[k]] = 16 + k
 
+    def pick(tile, octet):
+        index = orient_ref[pl.ds(octet * SUB * tiles + tile, SUB, stride=tiles), :]
+        low, high = index & (LANES - 1), index >> 7
+        values = [None] * 6
+        for table_tile in range(table_tiles):
+            here = high == table_tile
+            for which in range(6):
+                source = jnp.broadcast_to(
+                    trig_ref[
+                        which : which + 1, table_tile * LANES : (table_tile + 1) * LANES
+                    ],
+                    (SUB, LANES),
+                )
+                found = jnp.take_along_axis(source, low, axis=1, mode="promise_in_bounds")
+                values[which] = found if table_tile == 0 else jnp.where(here, found, values[which])
+        return values
+
     def one_tile(tile, unused):
         for octet in range(octets):
-            at = tile * octets + octet
-            bond = bond_matrix([picked_ref[which * len(groups) + at] for which in range(6)])
+            bond = bond_matrix(pick(tile, octet))
             mass = weight_ref[
                 octet * SUB : (octet + 1) * SUB, pl.ds(pl.multiple_of(tile * LANES, LANES), LANES)
             ].astype(jnp.float32)
@@ -366,10 +395,11 @@
         return unused
 
     lax.fori_loop(0, tiles, one_tile, 0)
+    for copy in copies[4:]:
+        copy.wait()
 
     slots = map_ref[...]
     half = cells // (cells // 32)
-    place_ref[...] = jnp.zeros_like(place_ref)
     for chunk in range(cells // half):
         wanted = rows_of((half, cells)) + chunk * half
         hit = jnp.where(jnp.broadcast_to(slots, (half, cells)) == wanted, 1.0, 0.0)
@@ -651,22 +681,31 @@
     tiles = cells // LANES
     octets = grains // SUB
     vmem = pl.BlockSpec(memory_space=pltpu.VMEM)
-    smem = pl.BlockSpec(memory_space=pltpu.SMEM)
+    hbm = pl.BlockSpec(memory_space=pltpu.HBM)
     f32 = jnp.float32
 
     send = pl.pallas_call(
         grain_kernel,
         out_shape=jax.ShapeDtypeStruct((devices, BLOCK_ROWS, LANES), f32),
-        in_specs=[smem] + [vmem] * 7,
+        in_specs=[hbm] * 8,
         out_specs=vmem,
         scratch_shapes=[
+            pltpu.SMEM((21,), f32),
+            pltpu.VMEM(euler_table.shape, f32),
+            pltpu.VMEM((grains * tiles, LANES), jnp.int32),
+            pltpu.VMEM((grains, cells), weight.dtype),
+            pltpu.VMEM((1, cells), jnp.int32),
+            pltpu.VMEM((SUB * 4, 8), f32),
+            pltpu.VMEM((3 * SUB * 4, 8), f32),
+            pltpu.VMEM((6 * SUB * 4, 8), f32),
             pltpu.VMEM((SUB, euler_table.shape[1]), f32),
-            pltpu.VMEM((6 * tiles * octets, SUB, LANES), f32),
             pltpu.VMEM((32, cells), f32),
             pltpu.VMEM((2 * cells, cells), jnp.bfloat16),
             pltpu.VMEM((22, SUB, LANES), f32),
+            pltpu.SemaphoreType.DMA((8,)),
         ],
-    )(
+        compiler_params=pltpu.CompilerParams(vmem_limit_bytes=8 * 2**20),
+    )(*[pltpu.with_memory_space_constraint(x, pltpu.HBM) for x in (
         crystal,
         euler_table,
         orient.reshape(grains * tiles, LANES),
@@ -675,7 +714,7 @@
         density.reshape(SUB * 4, 8),
         velocity.reshape(3 * SUB * 4, 8),
         stress.reshape(6 * SUB * 4, 8),
-    )
+    )])
     got = lax.all_to_all(send, ("gx", "gy", "ga"), split_axis=0, concat_axis=0, tiled=True)
     stiff, middle_stress, middle_velocity, wide_density = pl.pallas_call(
         first_step_kernel,
@@ -691,6 +730,7 @@
             pltpu.VMEM((FIELDS, 24, LANES), f32),
             pltpu.VMEM((3, 16, LANES), f32),
         ],
+        compiler_params=pltpu.CompilerParams(vmem_limit_bytes=8 * 2**20),
     )(got)
     pair = lax.ppermute(middle_stress, "gx", [(i, i ^ 1) for i in range(part_x)])
     swaps = [(i, i + 1) for i in range(1, part_x - 1, 2)]
@@ -702,6 +742,7 @@
         out_specs=vmem,
         scratch_shapes=[pltpu.VMEM((LANES, 24), f32)],
         cost_estimate=pl.CostEstimate(flops=100000, bytes_accessed=200000, transcendentals=0),
+        compiler_params=pltpu.CompilerParams(vmem_limit_bytes=8 * 2**20),
     )(stiff)
     new_velocity, new_stress = pl.pallas_call(
         functools.partial(last_step_kernel, bricks=part_x),
@@ -715,6 +756,7 @@
             pltpu.VMEM((6, 24, LANES), f32),
             pltpu.VMEM((3, 16, LANES), f32),
         ],
+        compiler_params=pltpu.CompilerParams(vmem_limit_bytes=8 * 2**20),
     )(middle_stress, pair, cross, middle_velocity, wide_density, stiff)
     return (
         stiffness.reshape(SUB, 4, 8, 21).transpose(3, 0, 1, 2),

time: 40 us -> 33 us (0.82)
  Pallas kernels: 11.7 us -> 5.73 us
  local copies, waits for them, and re-layouts: 0.6 us -> 0 us
    pallas_call x1, Pallas kernels: 5.74 us -> 3.3 us  [on_plane(): pl.pallas_call(grain_kernel, out_shape=jax.ShapeDtypeStruct((devices, BLO...]
    pallas_call x1, Pallas kernels: 2.18 us -> 0.51 us  [on_plane(): pl.pallas_call(first_step_kernel, out_shape=(jax.ShapeDtypeStruct((part_x...]
    pallas_call x1, Pallas kernels: 2.02 us -> 1.05 us  [on_plane(): pl.pallas_call(functools.partial(last_step_kernel, bricks=part_x), out_sh...]
    pallas_call x1, Pallas kernels: 1.76 us -> 0.87 us  [on_plane(): pl.pallas_call(stiffness_kernel, out_shape=jax.ShapeDtypeStruct((SUB * 4...]
    unnamed x4 -> x0, local copies, waits for them, and re-layouts: 0.6 us -> none
  transfers between devices with their start and end apart: 2 -> 2, of which waited for: 0 -> 0; matrix products, arithmetic and copies ran while one was open for 0% -> 0% of each run, Pallas kernels for 4% -> 3%
where the time goes in v2:
time: 33 us; the launch traced here: 32.8 us
  blocking collectives  23.4 us (71%)
  Pallas kernels  5.73 us (17%)
  starting transfers between devices  3 us (9%)
  between operations  0.66 us (2%)
    all_to_all x1, blocking collectives, on_plane(): lax.all_to_all(send, ('gx', 'gy', 'ga'), split_axis=0, concat_axis=0, til...  23.4 us
    pallas_call x1, Pallas kernels, on_plane(): pl.pallas_call(grain_kernel, out_shape=jax.ShapeDtypeStruct((devices, BLO...  3.3 us
    ppermute x1, starting transfers between devices, on_plane(): lax.ppermute(middle_stress, 'gx', [(i, i ^ 1) for i in range(part_x)])  2.34 us
    pallas_call x1, Pallas kernels, on_plane(): pl.pallas_call(functools.partial(last_step_kernel, bricks=part_x), out_sh...  1.05 us
    pallas_call x1, Pallas kernels, on_plane(): pl.pallas_call(stiffness_kernel, out_shape=jax.ShapeDtypeStruct((SUB * 4...  0.87 us
    ppermute x1, starting transfers between devices, on_plane(): lax.ppermute(middle_stress, 'gx', swaps + [(b, a) for a, b in swaps])  0.66 us
  transfers between devices with their start and end apart: 2, of which 0 were waited for; matrix products, arithmetic and copies ran while one was open for 0% of the time, Pallas kernels for 3%

profile of v2, /device:TPU:0, one launch (start us, length us, event | category | flops | bytes accessed | tf_op | source)
XLA Modules:
  0.0 32.8 jit_solution(18356405431140192656)
XLA Ops:
  0.6 3.3 %shard_map.103 = f32[32,32,128]{2,1,0:T(8,128)S(1)} custom-call(f32[21]{0:T(128)} %crystal_hbm.1, f32[3,2048]{1,0:T(4,128)} %euler_hbm.1, s32[64,128]{1,0:T(8,128)} %bitcast.14, bf16[16,512]{1,0:T(8,128)(2,1)} %bitcast.15, s32[1,512]{1,0:T(1,128)} %bitcast.17, f32[32,8]{1,0:T(8,128)} %bitcast.16, f32[96,8]{1,0:T(8,128)} %bitcast.13, f32[192,8]{1,0:T(8,128)} %bitcast.12), custom_call_target="tpu_custom_call" | custom-call | tf_op jit(solution)/shard_map/pallas_call | solution.py:687
  3.9 23.4 %all_to_all.5.got_ref = f32[32,32,128]{2,1,0:T(8,128)S(1)} all-to-all(f32[32,32,128]{2,1,0:T(8,128)S(1)} %shard_map.103), channel_id=1, replica_groups=mesh['gx'=8,'gy'=2,'ga'=2] {'gx','gy','ga'}, dimensions={0} | all-to-all | bytes 1048576 | tf_op jit(solution)/shard_map/all_to_all | solution.py:718
  27.4 0.5 %shard_map.104 = (f32[192,128]{1,0:T(8,128)S(1)}, f32[6,8,128]{2,1,0:T(8,128)S(1)}, f32[3,16,128]{2,1,0:T(8,128)S(1)}, f32[16,128]{1,0:T(8,128)S(1)}) custom-call(f32[32,32,128]{2,1,0:T(8,128)S(1)} %all_to_all.5.got_ref), custom_call_target="tpu_custom_call" | custom-call | tf_op jit(solution)/shard_map/pallas_call | solution.py:719
  27.9 0.7 %collective-permute-start.1 = (f32[6,8,128]{2,1,0:T(8,128)S(1)}, f32[6,8,128]{2,1,0:T(8,128)S(1)}, u32[]{:S(2)}, u32[]{:S(2)}) collective-permute-start(f32[6,8,128]{2,1,0:T(8,128)S(1)} %get-tuple-element.10.stress_ref), channel_id=1, source_target_pairs={{4,8},{12,16},{20,24},{8,4},{16,12},{24,20},{5,9},{13,17},{21,25},... | collective-permute-start | bytes 73736 | tf_op jit(solution)/shard_map/ppermute | solution.py:737
  28.5 2.3 %collective-permute-start = (f32[6,8,128]{2,1,0:T(8,128)S(1)}, f32[6,8,128]{2,1,0:T(8,128)S(1)}, u32[]{:S(2)}, u32[]{:S(2)}) collective-permute-start(f32[6,8,128]{2,1,0:T(8,128)S(1)} %get-tuple-element.10.stress_ref), channel_id=1, source_target_pairs={{0,4},{4,0},{8,12},{12,8},{16,20},{20,16},{24,28},{28,24},{1,5},{5... | collective-permute-start | bytes 73736 | tf_op jit(solution)/shard_map/ppermute | solution.py:735
  30.9 0.9 %shard_map.105 = f32[256,21]{1,0:T(8,128)} custom-call(f32[192,128]{1,0:T(8,128)S(1)} %get-tuple-element.9.stiff_ref), custom_call_target="tpu_custom_call" | custom-call | flops 100000 | bytes 200000 | tf_op jit(solution)/shard_map/pallas_call | solution.py:738
  31.8 0.0 collective-permute-done.1.cross_ref
  31.8 0.0 collective-permute-done.pair_ref
  31.8 1.0 %shard_map.106 = (f32[96,8]{1,0:T(8,128)}, f32[192,8]{1,0:T(8,128)}) custom-call(f32[6,8,128]{2,1,0:T(8,128)S(1)} %get-tuple-element.10.stress_ref, f32[6,8,128]{2,1,0:T(8,128)S(1)} %collective-permute-done.pair_ref, f32[6,8,128]{2,1,0:T(8,128)S(1)} %collective-permute-done.1.cross_ref, f32[3,16,128]{2,1,0:T(8,128)S(1)} %get-tuple-element.11.velocity_ref, ...), custom_call_target="tpu_custom_call" | custom-call | tf_op jit(solution)/shard_map/pallas_call | solution.py:747
Async XLA Ops:
  27.9 3.9 %collective-permute-start.1 = (f32[6,8,128]{2,1,0:T(8,128)S(1)}, f32[6,8,128]{2,1,0:T(8,128)S(1)}, u32[]{:S(2)}, u32[]{:S(2)}) collective-permute-start(f32[6,8,128]{2,1,0:T(8,128)S(1)} %get-tuple-element.10.stress_ref), channel_id=1, source_target_pairs={{4,8},{12,16},{20,24},{8,4},{16,12},{24,20},{5,9},{13,17},{21,25},... | collective-permute-start | bytes 73736 | tf_op jit(solution)/shard_map/ppermute | solution.py:737
  28.5 3.2 %collective-permute-start = (f32[6,8,128]{2,1,0:T(8,128)S(1)}, f32[6,8,128]{2,1,0:T(8,128)S(1)}, u32[]{:S(2)}, u32[]{:S(2)}) collective-permute-start(f32[6,8,128]{2,1,0:T(8,128)S(1)} %get-tuple-element.10.stress_ref), channel_id=1, source_target_pairs={{0,4},{4,0},{8,12},{12,8},{16,20},{20,16},{24,28},{28,24},{1,5},{5... | collective-permute-start | bytes 73736 | tf_op jit(solution)/shard_map/ppermute | solution.py:735

commit v3 on v2

--- a/solution.py
+++ b/solution.py
@@ -222,8 +222,10 @@
 
 SUB = 8
 LANES = 128
-BLOCK_ROWS = 32
+SUM_ROWS = 11
+BLOCK_ROWS = 21
 FIELDS = 10
+HALF = FIELDS // 2
 LOW_ROWS = tuple(range(8)) + (16, 17, 18)
 HIGH_ROWS = tuple(range(8, 16)) + (19, 20, 21)
 
@@ -316,7 +318,7 @@
     tiles = cells // LANES
     octets = grains // SUB
     table_tiles = euler_ref.shape[1] // LANES
-    destinations = send_ref.shape[0]
+    destinations = send_ref.shape[0] // BLOCK_ROWS
 
     copies = [
         pltpu.make_async_copy(source, target, arrived.at[at])
@@ -417,8 +419,6 @@
     placed = placed[0:32] + placed[32:64] + placed[64:96]
 
     own = row_part * 2 + layer
-    lane = lanes_of((SUB, LANES))
-    row = rows_of((SUB, LANES))
 
     def field_rows(component, y):
         if component < 6:
@@ -438,26 +438,26 @@
         return into
 
     nothing = jnp.zeros((SUB, LANES), jnp.float32)
-    group_one, group_two, tail_low, tail_high = nothing, nothing, nothing, nothing
-    for slot in range(4):
-        group_one = spread(slot, slot, group_one)
-        group_two = spread(4 + slot, slot, group_two)
-    tail_low = spread(9, 2, spread(8, 0, tail_low))
-    tail_high = spread(9, 3, spread(8, 1, tail_high))
-    tail = pltpu.roll(tail_low, 4, 0) + tail_high
+    groups, tails = [], []
+    for half in range(2):
+        group, tail = nothing, nothing
+        for slot in range(4):
+            group = spread(half * HALF + slot, slot, group)
+            piece = spread(half * HALF + 4, slot, nothing)
+            tail = tail + (piece if slot == 0 else pltpu.roll(piece, SUB - 2 * slot, 0))
+        groups.append(group)
+        tails.append(tail[0:2])
 
     shift = 32 + row_part * 64
     for brick in range(destinations // 4):
         low_half = placed[0:16, brick * LANES : (brick + 1) * LANES]
         high_half = placed[16:32, brick * LANES : (brick + 1) * LANES]
         packed = low_half + pltpu.roll(high_half, shift, 1)
-        last = jnp.where(row < 4, packed[8:16], tail)
         for inner in range(4):
-            at = brick * 4 + inner
-            send_ref[at, 0:8, :] = packed[0:8]
-            send_ref[at, 8:16, :] = last
-            send_ref[at, 16:24, :] = group_one
-            send_ref[at, 24:32, :] = group_two
+            at = (brick * 4 + inner) * BLOCK_ROWS
+            send_ref[at : at + SUM_ROWS, :] = packed[0:SUM_ROWS]
+            send_ref[at + SUM_ROWS : at + SUM_ROWS + SUB, :] = groups[brick % 2]
+            send_ref[at + SUM_ROWS + SUB : at + BLOCK_ROWS, :] = tails[brick % 2]
 
 
 def plane_derivative(field, dim, lane):
@@ -538,31 +538,22 @@
     return ((brick > 0) | (place >= 0)) & ((brick < bricks - 1) | (place < SUB))
 
 
-def first_step_kernel(
-    got_ref, stiff_ref, stress_ref, velocity_ref, density_ref, wide_ref, moving_ref
-):
+def field_kernel(got_ref, half_ref):
     brick = lax.axis_index("gx")
-    bricks = got_ref.shape[0] // 4
-    lane = lanes_of((SUB, LANES))
-    row = rows_of((SUB, LANES))
-
-    lane_two = lanes_of((16, LANES))
-    own_slot = (lane_two // 32) % 2 == 0
-    for p in range(bricks):
-        zero = got_ref[p * 4, 0:16, :] + got_ref[p * 4 + 1, 0:16, :]
-        one = got_ref[p * 4 + 2, 0:16, :] + got_ref[p * 4 + 3, 0:16, :]
-        low = jnp.where(own_slot, zero, one)
-        high = jnp.where(own_slot, one, zero)
-        high = jnp.where(own_slot, pltpu.roll(high, LANES - 32, 1), pltpu.roll(high, 32, 1))
-        total = jnp.broadcast_to(high[10:11], (SUB, LANES))
-        stiff_ref[p * 24 : p * 24 + 8, :] = low[0:8] / total
-        stiff_ref[p * 24 + 8 : p * 24 + 16, :] = high[0:8] / total
-        last = jnp.where(row < 3, low[8:16], pltpu.roll(high[8:16], 3, 0))
-        stiff_ref[p * 24 + 16 : p * 24 + 24, :] = last / total
-
-    kind = (lane // 64) * 2 + (lane // 8) % 2
-
-    def settle(value, slot):
+    bricks = got_ref.shape[0] // BLOCK_ROWS // 4
+
+    def collect(source, offset, count, slot):
+        lane = lanes_of((count, LANES))
+        kind = (lane // 64) * 2 + (lane // 8) % 2
+        pieces = [
+            got_ref[pl.ds((source * 4 + (q ^ slot)) * BLOCK_ROWS + offset, count), :]
+            for q in range(4)
+        ]
+        value = jnp.where(
+            kind < 2,
+            jnp.where(kind == 0, pieces[0], pieces[1]),
+            jnp.where(kind == 2, pieces[2], pieces[3]),
+        )
         if slot & 1:
             value = jnp.where(
                 (lane // 8) % 2 == 0,
@@ -573,38 +564,59 @@
             value = pltpu.roll(value, 64, 1)
         return value
 
-    for side in range(3):
-        source = jnp.clip(brick + side - 1, 0, bricks - 1)
-        valid = source == brick + side - 1
-
-        def collect(rows, slot):
-            pieces = [got_ref[source * 4 + (q ^ slot), rows : rows + 8, :] for q in range(4)]
-            value = jnp.where(
-                kind < 2,
-                jnp.where(kind == 0, pieces[0], pieces[1]),
-                jnp.where(kind == 2, pieces[2], pieces[3]),
-            )
-            return settle(value, slot)
-
-        def keep(component, value):
-            value = jnp.where(valid, value, 1.0 if component == 9 else 0.0)
-            wide_ref[component, side * SUB : (side + 1) * SUB, :] = value
-
+    for side in range(4):
+        wanted = (brick // 2) * 2 + side - 1
+        source = jnp.clip(wanted, 0, bricks - 1)
+        valid = source == wanted
+        first = side * SUB
         for slot in range(4):
-            keep(slot, collect(16, slot))
-            keep(4 + slot, collect(24, slot))
-        for component in (8, 9):
-            slot = (component - 8) * 2
-            upper = pltpu.roll(collect(8, slot), 4, 0)
-            keep(component, jnp.where(row < 4, upper, collect(8, slot + 1)))
-
-    density = wide_ref[9, 4:20, :]
+            value = collect(source, SUM_ROWS, SUB, slot)
+            half_ref[slot, first : first + SUB, :] = jnp.where(valid, value, 0.0)
+            value = collect(source, SUM_ROWS + SUB, 2, slot)
+            half_ref[4, first + 2 * slot : first + 2 * slot + 2, :] = jnp.where(valid, value, 0.0)
+
+
+def sums_kernel(got_ref, stiff_ref):
+    row = rows_of((SUB, LANES))
+    own_slot = (lanes_of((SUM_ROWS, LANES)) // 32) % 2 == 0
+    for p in range(got_ref.shape[0] // BLOCK_ROWS // 4):
+        zero, one = [
+            got_ref[at : at + SUM_ROWS, :] + got_ref[at + BLOCK_ROWS : at + BLOCK_ROWS + SUM_ROWS, :]
+            for at in (p * 4 * BLOCK_ROWS, (p * 4 + 2) * BLOCK_ROWS)
+        ]
+        low = jnp.where(own_slot, zero, one)
+        high = jnp.where(own_slot, one, zero)
+        high = jnp.where(own_slot, pltpu.roll(high, LANES - 32, 1), pltpu.roll(high, 32, 1))
+        total = jnp.broadcast_to(high[10:11], (SUB, LANES))
+        stiff_ref[p * 24 : p * 24 + 8, :] = low[0:8] / total
+        stiff_ref[p * 24 + 8 : p * 24 + 16, :] = high[0:8] / total
+        stiff_ref[p * 24 + 16 : p * 24 + 19, :] = low[8:11] / total[0:3]
+        stiff_ref[p * 24 + 19 : p * 24 + 22, :] = high[8:11] / total[0:3]
+
+
+def first_step_kernel(
+    own_ref,
+    other_ref,
+    stiff_ref,
+    stress_ref,
+    velocity_ref,
+    density_ref,
+    wide_ref,
+    moving_ref,
+    *,
+    bricks,
+):
+    brick = lax.axis_index("gx")
+    odd = brick % 2
+    rows = pl.ds(pl.multiple_of(odd * SUB, SUB), 24)
+    for at in range(HALF):
+        wide_ref[odd * HALF + at] = own_ref[at, rows, :]
+        wide_ref[(1 - odd) * HALF + at] = other_ref[at, rows, :]
+    inside = inside_rows(brick, bricks)
+    density = jnp.where(inside, wide_ref[9, 4:20, :], 1.0)
     density_ref[...] = density
     fresh = velocity_update(
-        wide_ref,
-        [wide_ref[6 + at, 4:20, :] for at in range(3)],
-        density,
-        inside_rows(brick, bricks),
+        wide_ref, [wide_ref[6 + at, 4:20, :] for at in range(3)], density, inside
     )
     for at in range(3):
         velocity_ref[at] = fresh[at]
@@ -686,7 +698,7 @@
 
     send = pl.pallas_call(
         grain_kernel,
-        out_shape=jax.ShapeDtypeStruct((devices, BLOCK_ROWS, LANES), f32),
+        out_shape=jax.ShapeDtypeStruct((devices * BLOCK_ROWS, LANES), f32),
         in_specs=[hbm] * 8,
         out_specs=vmem,
         scratch_shapes=[
@@ -715,24 +727,47 @@
         velocity.reshape(3 * SUB * 4, 8),
         stress.reshape(6 * SUB * 4, 8),
     )])
-    got = lax.all_to_all(send, ("gx", "gy", "ga"), split_axis=0, concat_axis=0, tiled=True)
-    stiff, middle_stress, middle_velocity, wide_density = pl.pallas_call(
-        first_step_kernel,
+    got = lax.all_to_all(
+        send.reshape(devices, 1, BLOCK_ROWS * LANES),
+        ("gx", "gy", "ga"),
+        split_axis=0,
+        concat_axis=0,
+        tiled=True,
+    ).reshape(devices * BLOCK_ROWS, LANES)
+    small = pltpu.CompilerParams(vmem_limit_bytes=8 * 2**20)
+    own_half = pl.pallas_call(
+        field_kernel,
+        out_shape=jax.ShapeDtypeStruct((HALF, 4 * SUB, LANES), f32),
+        in_specs=[vmem],
+        out_specs=vmem,
+        compiler_params=small,
+    )(got)
+    partners = [(i, i ^ 1) for i in range(part_x)]
+    other_half = lax.ppermute(own_half, "gx", partners)
+    stiff = pl.pallas_call(
+        sums_kernel,
+        out_shape=jax.ShapeDtypeStruct((part_x * 24, LANES), f32),
+        in_specs=[vmem],
+        out_specs=vmem,
+        cost_estimate=pl.CostEstimate(flops=100000, bytes_accessed=200000, transcendentals=0),
+        compiler_params=small,
+    )(got)
+    middle_stress, middle_velocity, wide_density = pl.pallas_call(
+        functools.partial(first_step_kernel, bricks=part_x),
         out_shape=(
-            jax.ShapeDtypeStruct((part_x * 24, LANES), f32),
             jax.ShapeDtypeStruct((6, SUB, LANES), f32),
             jax.ShapeDtypeStruct((3, 16, LANES), f32),
             jax.ShapeDtypeStruct((16, LANES), f32),
         ),
-        in_specs=[vmem],
-        out_specs=(vmem,) * 4,
+        in_specs=[vmem] * 3,
+        out_specs=(vmem,) * 3,
         scratch_shapes=[
             pltpu.VMEM((FIELDS, 24, LANES), f32),
             pltpu.VMEM((3, 16, LANES), f32),
         ],
-        compiler_params=pltpu.CompilerParams(vmem_limit_bytes=8 * 2**20),
-    )(got)
-    pair = lax.ppermute(middle_stress, "gx", [(i, i ^ 1) for i in range(part_x)])
+        compiler_params=small,
+    )(own_half, other_half, stiff)
+    pair = lax.ppermute(middle_stress, "gx", partners)
     swaps = [(i, i + 1) for i in range(1, part_x - 1, 2)]
     cross = lax.ppermute(middle_stress, "gx", swaps + [(b, a) for a, b in swaps])
     stiffness = pl.pallas_call(

time: 33 us -> 31.5 us (0.955)
  the two profiles are of different devices: /device:TPU:0 before, /device:TPU:1 now
where the time goes in v3:
time: 31.5 us; the launch traced here: 31.4 us
  blocking collectives  18.1 us (57%)
  Pallas kernels  5.8 us (18%)
  starting transfers between devices  4.4 us (14%)
  waiting for transfers between devices  2.34 us (7%)
  between operations  0.67 us (2%)
    all_to_all x1, blocking collectives, on_plane(): lax.all_to_all(send.reshape(devices, 1, BLOCK_ROWS * LANES), ('gx', 'gy',...  18.1 us
    pallas_call x1, Pallas kernels, on_plane(): pl.pallas_call(grain_kernel, out_shape=jax.ShapeDtypeStruct((devices * BL...  3.29 us
    ppermute x1, starting transfers between devices, on_plane(): lax.ppermute(middle_stress, 'gx', swaps + [(b, a) for a, b in swaps])  2.66 us
    ppermute x1, starting transfers between devices, on_plane(): other_half = lax.ppermute(own_half, 'gx', partners)  1.67 us
    ppermute x1, waiting for transfers between devices, on_plane(): lax.ppermute(middle_stress, 'gx', swaps + [(b, a) for a, b in swaps])  1.52 us
    pallas_call x1, Pallas kernels, on_plane(): pl.pallas_call(functools.partial(last_step_kernel, bricks=part_x), out_sh...  1.05 us
    pallas_call x1, Pallas kernels, on_plane(): pl.pallas_call(stiffness_kernel, out_shape=jax.ShapeDtypeStruct((SUB * 4...  0.87 us
    ppermute x1, waiting for transfers between devices, on_plane(): other_half = lax.ppermute(own_half, 'gx', partners)  0.81 us
  transfers between devices with their start and end apart: 3, of which 2 were waited for; matrix products, arithmetic and copies ran while one was open for 0% of the time, Pallas kernels for 3%

profile of v3, /device:TPU:1, one launch (start us, length us, event | category | flops | bytes accessed | tf_op | source)
XLA Modules:
  0.0 31.4 jit_solution(18343611141921412547)
XLA Ops:
  0.6 3.3 %shard_map.103 = f32[672,128]{1,0:T(8,128)S(1)} custom-call(f32[21]{0:T(128)} %crystal_hbm.1, f32[3,2048]{1,0:T(4,128)} %euler_hbm.1, s32[64,128]{1,0:T(8,128)} %bitcast.19, bf16[16,512]{1,0:T(8,128)(2,1)} %bitcast.20, s32[1,512]{1,0:T(1,128)} %bitcast.22, f32[32,8]{1,0:T(8,128)} %bitcast.21, f32[96,8]{1,0:T(8,128)} %bitcast.18, f32[192,8]{1,0:T(8,128)} %bitcast.17), custom_call_target="tpu_custom_call" | custom-call | tf_op jit(solution)/shard_map/pallas_call | solution.py:699
  3.9 18.1 %all_to_all.5 = f32[32,1,2688]{2,1,0:T(1,128)S(1)} all-to-all(f32[32,1,2688]{2,1,0:T(1,128)S(1)} %bitcast.15), channel_id=1, replica_groups=mesh['gx'=8,'gy'=2,'ga'=2] {'gx','gy','ga'}, dimensions={0} | all-to-all | bytes 688128 | tf_op jit(solution)/shard_map/all_to_all | solution.py:730
  22.1 0.2 shard_map.106.own_ref
  22.2 1.7 %collective-permute-start = (f32[5,32,128]{2,1,0:T(8,128)S(1)}, f32[5,32,128]{2,1,0:T(8,128)S(1)}, u32[]{:S(2)}, u32[]{:S(2)}) collective-permute-start(f32[5,32,128]{2,1,0:T(8,128)S(1)} %shard_map.106.own_ref), channel_id=1, source_target_pairs={{0,4},{4,0},{8,12},{12,8},{16,20},{20,16},{24,28},{28,24},{1,5},{5... | collective-permute-start | bytes 245768 | tf_op jit(solution)/shard_map/ppermute | solution.py:746
  23.9 0.1 shard_map.104.stiff_ref
  24.0 0.8 %collective-permute-done.other_ref = f32[5,32,128]{2,1,0:T(8,128)S(1)} collective-permute-done((f32[5,32,128]{2,1,0:T(8,128)S(1)}, f32[5,32,128]{2,1,0:T(8,128)S(1)}, u32[]{:S(2)}, u32[]{:S(2)}) %collective-permute-start) | collective-permute-done | bytes 81952 | tf_op jit(solution)/shard_map/ppermute | solution.py:746
  24.8 0.3 shard_map.107
  25.2 2.7 %collective-permute-start.2 = (f32[6,8,128]{2,1,0:T(8,128)S(1)}, f32[6,8,128]{2,1,0:T(8,128)S(1)}, u32[]{:S(2)}, u32[]{:S(2)}) collective-permute-start(f32[6,8,128]{2,1,0:T(8,128)S(1)} %get-tuple-element.8.stress_ref), channel_id=1, source_target_pairs={{4,8},{12,16},{20,24},{8,4},{16,12},{24,20},{5,9},{13,17},{21,25},... | collective-permute-start | bytes 73736 | tf_op jit(solution)/shard_map/ppermute | solution.py:772
  27.8 0.1 collective-permute-start.1
  27.9 0.9 %shard_map.105 = f32[256,21]{1,0:T(8,128)} custom-call(f32[192,128]{1,0:T(8,128)S(1)} %shard_map.104.stiff_ref), custom_call_target="tpu_custom_call" | custom-call | flops 100000 | bytes 200000 | tf_op jit(solution)/shard_map/pallas_call | solution.py:773
  28.8 1.5 %collective-permute-done.2.cross_ref = f32[6,8,128]{2,1,0:T(8,128)S(1)} collective-permute-done((f32[6,8,128]{2,1,0:T(8,128)S(1)}, f32[6,8,128]{2,1,0:T(8,128)S(1)}, u32[]{:S(2)}, u32[]{:S(2)}) %collective-permute-start.2) | collective-permute-done | bytes 24608 | tf_op jit(solution)/shard_map/ppermute | solution.py:772
  30.3 0.0 collective-permute-done.1.pair_ref
  30.3 1.0 %shard_map.108 = (f32[96,8]{1,0:T(8,128)}, f32[192,8]{1,0:T(8,128)}) custom-call(f32[6,8,128]{2,1,0:T(8,128)S(1)} %get-tuple-element.8.stress_ref, f32[6,8,128]{2,1,0:T(8,128)S(1)} %collective-permute-done.1.pair_ref, f32[6,8,128]{2,1,0:T(8,128)S(1)} %collective-permute-done.2.cross_ref, f32[3,16,128]{2,1,0:T(8,128)S(1)} %get-tuple-element.9.velocity_ref, ...), custom_call_target="tpu_custom_call" | custom-call | tf_op jit(solution)/shard_map/pallas_call | solution.py:782
Async XLA Ops:
  22.2 2.6 %collective-permute-start = (f32[5,32,128]{2,1,0:T(8,128)S(1)}, f32[5,32,128]{2,1,0:T(8,128)S(1)}, u32[]{:S(2)}, u32[]{:S(2)}) collective-permute-start(f32[5,32,128]{2,1,0:T(8,128)S(1)} %shard_map.106.own_ref), channel_id=1, source_target_pairs={{0,4},{4,0},{8,12},{12,8},{16,20},{20,16},{24,28},{28,24},{1,5},{5... | collective-permute-start | bytes 245768 | tf_op jit(solution)/shard_map/ppermute | solution.py:746
  25.2 5.1 %collective-permute-start.2 = (f32[6,8,128]{2,1,0:T(8,128)S(1)}, f32[6,8,128]{2,1,0:T(8,128)S(1)}, u32[]{:S(2)}, u32[]{:S(2)}) collective-permute-start(f32[6,8,128]{2,1,0:T(8,128)S(1)} %get-tuple-element.8.stress_ref), channel_id=1, source_target_pairs={{4,8},{12,16},{20,24},{8,4},{16,12},{24,20},{5,9},{13,17},{21,25},... | collective-permute-start | bytes 73736 | tf_op jit(solution)/shard_map/ppermute | solution.py:772
  27.8 2.5 %collective-permute-start.1 = (f32[6,8,128]{2,1,0:T(8,128)S(1)}, f32[6,8,128]{2,1,0:T(8,128)S(1)}, u32[]{:S(2)}, u32[]{:S(2)}) collective-permute-start(f32[6,8,128]{2,1,0:T(8,128)S(1)} %get-tuple-element.8.stress_ref), channel_id=1, source_target_pairs={{0,4},{4,0},{8,12},{12,8},{16,20},{20,16},{24,28},{28,24},{1,5},{5... | collective-permute-start | bytes 73736 | tf_op jit(solution)/shard_map/ppermute | solution.py:770

commit v4 on v3

--- a/solution.py
+++ b/solution.py
@@ -223,7 +223,12 @@
 SUB = 8
 LANES = 128
 SUM_ROWS = 11
-BLOCK_ROWS = 21
+EDGE_ROWS = 6
+FIELD_AT = SUM_ROWS + EDGE_ROWS
+BLOCK_ROWS = FIELD_AT + 10
+EDGE_AT = 192
+WIDE_AT = EDGE_AT + 128
+WIDE_ROWS = 48
 FIELDS = 10
 HALF = FIELDS // 2
 LOW_ROWS = tuple(range(8)) + (16, 17, 18)
@@ -252,6 +257,17 @@
 
 def rows_of(shape):
     return lax.broadcasted_iota(jnp.int32, shape, len(shape) - 2)
+
+
+def opposite_class(value, lane):
+    value = jnp.where(
+        (lane // 8) % 2 == 0, pltpu.roll(value, LANES - 8, 1), pltpu.roll(value, 8, 1)
+    )
+    return pltpu.roll(value, LANES // 2, 1)
+
+
+def near_lanes(lane, row_half, layer):
+    return (lane // 64 == row_half) | ((lane // 8) % 2 == layer)
 
 
 def bond_matrix(trig):
@@ -449,15 +465,35 @@
         tails.append(tail[0:2])
 
     shift = 32 + row_part * 64
-    for brick in range(destinations // 4):
-        low_half = placed[0:16, brick * LANES : (brick + 1) * LANES]
-        high_half = placed[16:32, brick * LANES : (brick + 1) * LANES]
-        packed = low_half + pltpu.roll(high_half, shift, 1)
+    bricks = destinations // 4
+    lane = lanes_of((SUB, LANES))
+    upper = lax.axis_index("gx") >= SUB // 2
+    own_sums, edge_sums = [], []
+    for brick in range(bricks):
+        halves = [
+            placed[at : at + 16, brick * LANES : (brick + 1) * LANES] for at in (0, 16)
+        ]
+        own_sums.append(halves[0] + pltpu.roll(halves[1], shift, 1))
+        edge_sums.append(
+            [
+                half[0:8] + pltpu.roll(pltpu.roll(half, 16 - EDGE_ROWS, 0)[0:8], shift, 1)
+                for half in halves
+            ]
+        )
+    for brick in range(bricks):
+        side = brick % 2
+        before, after = brick - side - 1, brick - side + 2
+        before = edge_sums[before][side] if before >= 0 else nothing
+        after = edge_sums[after][side] if after < bricks else nothing
+        near = jnp.where(upper, before, after)
+        far = opposite_class(jnp.where(upper, after, before), lane)
         for inner in range(4):
             at = (brick * 4 + inner) * BLOCK_ROWS
-            send_ref[at : at + SUM_ROWS, :] = packed[0:SUM_ROWS]
-            send_ref[at + SUM_ROWS : at + SUM_ROWS + SUB, :] = groups[brick % 2]
-            send_ref[at + SUM_ROWS + SUB : at + BLOCK_ROWS, :] = tails[brick % 2]
+            edge = jnp.where(near_lanes(lane, inner // 2, inner % 2), near, far)
+            send_ref[at : at + SUM_ROWS, :] = own_sums[brick][0:SUM_ROWS]
+            send_ref[at + SUM_ROWS : at + FIELD_AT, :] = edge[0:EDGE_ROWS]
+            send_ref[at + FIELD_AT : at + FIELD_AT + SUB, :] = groups[side]
+            send_ref[at + FIELD_AT + SUB : at + BLOCK_ROWS, :] = tails[side]
 
 
 def plane_derivative(field, dim, lane):
@@ -485,8 +521,7 @@
     return total
 
 
-def velocity_update(wide_stress, old_velocity, density, inside):
-    count = 16
+def velocity_update(wide_stress, old_velocity, density, inside, count):
     lane = lanes_of((count, LANES))
 
     def along(component, dim):
@@ -507,15 +542,15 @@
     ]
 
 
-def stress_update(wide_velocity, old_stress, stiff):
+def stress_update(wide_velocity, start, old_stress, stiff):
     lane = lanes_of((SUB, LANES))
 
     def along(component, dim):
         if dim == 0:
             return row_derivative(
-                lambda at, size: wide_velocity[component, at : at + size, :], 4, SUB
+                lambda at, size: wide_velocity[component, pl.ds(at, size), :], start, SUB
             )
-        return plane_derivative(wide_velocity[component, 4 : 4 + SUB, :], dim, lane)
+        return plane_derivative(wide_velocity[component, pl.ds(start, SUB), :], dim, lane)
 
     strain = [
         along(0, 0),
@@ -533,14 +568,40 @@
     ]
 
 
-def inside_rows(brick, bricks):
-    place = rows_of((16, LANES)) - 4
-    return ((brick > 0) | (place >= 0)) & ((brick < bricks - 1) | (place < SUB))
-
-
-def field_kernel(got_ref, half_ref):
+def inside_rows(brick, bricks, margin, count):
+    place = rows_of((count, LANES)) - margin + brick * SUB
+    return (place >= 0) & (place < bricks * SUB)
+
+
+def unpack_kernel(got_ref, out_ref):
     brick = lax.axis_index("gx")
     bricks = got_ref.shape[0] // BLOCK_ROWS // 4
+
+    def by_slot(zero, one):
+        first_slot = (lanes_of(zero.shape) // 32) % 2 == 0
+        low = jnp.where(first_slot, zero, one)
+        high = jnp.where(first_slot, one, zero)
+        high = jnp.where(first_slot, pltpu.roll(high, LANES - 32, 1), pltpu.roll(high, 32, 1))
+        return low, high
+
+    for p in range(bricks):
+
+        def both_layers(part, offset, count):
+            at = (p * 4 + part * 2) * BLOCK_ROWS + offset
+            return got_ref[at : at + count, :] + got_ref[at + BLOCK_ROWS : at + BLOCK_ROWS + count, :]
+
+        low, high = by_slot(both_layers(0, 0, SUM_ROWS), both_layers(1, 0, SUM_ROWS))
+        total = jnp.broadcast_to(high[10:11], (SUB, LANES))
+        out_ref[p * 24 : p * 24 + 8, :] = low[0:8] / total
+        out_ref[p * 24 + 8 : p * 24 + 16, :] = high[0:8] / total
+        out_ref[p * 24 + 16 : p * 24 + 19, :] = low[8:11] / total[0:3]
+        out_ref[p * 24 + 19 : p * 24 + 22, :] = high[8:11] / total[0:3]
+        low, high = by_slot(
+            both_layers(0, SUM_ROWS, EDGE_ROWS), both_layers(1, SUM_ROWS, EDGE_ROWS)
+        )
+        at = EDGE_AT + p * 16
+        out_ref[at : at + EDGE_ROWS, :] = low
+        out_ref[at + EDGE_ROWS : at + SUM_ROWS, :] = high[0 : SUM_ROWS - EDGE_ROWS]
 
     def collect(source, offset, count, slot):
         lane = lanes_of((count, LANES))
@@ -564,70 +625,17 @@
             value = pltpu.roll(value, 64, 1)
         return value
 
-    for side in range(4):
-        wanted = (brick // 2) * 2 + side - 1
+    for side in range(WIDE_ROWS // SUB):
+        wanted = (brick // 2) * 2 + side - 2
         source = jnp.clip(wanted, 0, bricks - 1)
         valid = source == wanted
-        first = side * SUB
         for slot in range(4):
-            value = collect(source, SUM_ROWS, SUB, slot)
-            half_ref[slot, first : first + SUB, :] = jnp.where(valid, value, 0.0)
-            value = collect(source, SUM_ROWS + SUB, 2, slot)
-            half_ref[4, first + 2 * slot : first + 2 * slot + 2, :] = jnp.where(valid, value, 0.0)
-
-
-def sums_kernel(got_ref, stiff_ref):
-    row = rows_of((SUB, LANES))
-    own_slot = (lanes_of((SUM_ROWS, LANES)) // 32) % 2 == 0
-    for p in range(got_ref.shape[0] // BLOCK_ROWS // 4):
-        zero, one = [
-            got_ref[at : at + SUM_ROWS, :] + got_ref[at + BLOCK_ROWS : at + BLOCK_ROWS + SUM_ROWS, :]
-            for at in (p * 4 * BLOCK_ROWS, (p * 4 + 2) * BLOCK_ROWS)
-        ]
-        low = jnp.where(own_slot, zero, one)
-        high = jnp.where(own_slot, one, zero)
-        high = jnp.where(own_slot, pltpu.roll(high, LANES - 32, 1), pltpu.roll(high, 32, 1))
-        total = jnp.broadcast_to(high[10:11], (SUB, LANES))
-        stiff_ref[p * 24 : p * 24 + 8, :] = low[0:8] / total
-        stiff_ref[p * 24 + 8 : p * 24 + 16, :] = high[0:8] / total
-        stiff_ref[p * 24 + 16 : p * 24 + 19, :] = low[8:11] / total[0:3]
-        stiff_ref[p * 24 + 19 : p * 24 + 22, :] = high[8:11] / total[0:3]
-
-
-def first_step_kernel(
-    own_ref,
-    other_ref,
-    stiff_ref,
-    stress_ref,
-    velocity_ref,
-    density_ref,
-    wide_ref,
-    moving_ref,
-    *,
-    bricks,
-):
-    brick = lax.axis_index("gx")
-    odd = brick % 2
-    rows = pl.ds(pl.multiple_of(odd * SUB, SUB), 24)
-    for at in range(HALF):
-        wide_ref[odd * HALF + at] = own_ref[at, rows, :]
-        wide_ref[(1 - odd) * HALF + at] = other_ref[at, rows, :]
-    inside = inside_rows(brick, bricks)
-    density = jnp.where(inside, wide_ref[9, 4:20, :], 1.0)
-    density_ref[...] = density
-    fresh = velocity_update(
-        wide_ref, [wide_ref[6 + at, 4:20, :] for at in range(3)], density, inside
-    )
-    for at in range(3):
-        velocity_ref[at] = fresh[at]
-        moving_ref[at] = fresh[at]
-    fresh = stress_update(
-        moving_ref,
-        [wide_ref[at, 8:16, :] for at in range(6)],
-        lambda pair: stiff_ref[pl.ds(pair, SUB, stride=24), :],
-    )
-    for at in range(6):
-        stress_ref[at] = fresh[at]
+            at = WIDE_AT + slot * WIDE_ROWS + side * SUB
+            value = collect(source, FIELD_AT, SUB, slot)
+            out_ref[at : at + SUB, :] = jnp.where(valid, value, 0.0)
+            at = WIDE_AT + 4 * WIDE_ROWS + side * SUB + 2 * slot
+            value = collect(source, FIELD_AT + SUB, 2, slot)
+            out_ref[at : at + 2, :] = jnp.where(valid, value, 0.0)
 
 
 def stiffness_kernel(stiff_ref, out_ref, turned_ref):
@@ -639,41 +647,83 @@
             out_ref[p * 32 + y * 8 : p * 32 + y * 8 + 8, :] = turned_ref[rows, 0:21]
 
 
-def last_step_kernel(
-    stress_ref,
-    pair_ref,
-    cross_ref,
-    velocity_ref,
-    density_ref,
-    stiff_ref,
+def steps_kernel(
+    own_ref,
+    other_ref,
     out_velocity_ref,
     out_stress_ref,
     wide_ref,
-    moving_ref,
+    edge_ref,
+    first_velocity_ref,
+    first_stress_ref,
+    last_velocity_ref,
     *,
     bricks,
 ):
     brick = lax.axis_index("gx")
-    even = brick % 2 == 0
-    for at in range(6):
-        pair, cross = pair_ref[at], cross_ref[at]
-        wide_ref[at, 0:8, :] = jnp.where(even, cross, pair)
-        wide_ref[at, 8:16, :] = stress_ref[at]
-        wide_ref[at, 16:24, :] = jnp.where(even, pair, cross)
+    row_part, layer = lax.axis_index("gy"), lax.axis_index("ga")
+    odd = brick % 2
+    lane = lanes_of((SUB, LANES))
+    row = rows_of((SUB, LANES))
+
+    for at in range(HALF):
+        rows = pl.ds(pl.multiple_of(WIDE_AT + at * WIDE_ROWS + odd * SUB, SUB), 5 * SUB)
+        wide_ref[odd * HALF + at] = own_ref[rows, :]
+        wide_ref[(1 - odd) * HALF + at] = other_ref[rows, :]
+
+    edge_valid = jnp.where(odd == 0, brick - 1, brick + 1)
+    edge_valid = (edge_valid >= 0) & (edge_valid < bricks)
+    near_row = jnp.where(odd == 0, row, SUB - 1 - row) >= SUB // 2
+    own_lane = (lane // 64 == row_part) & ((lane // 8) % 2 == layer)
+    usable = (own_lane | (near_row & near_lanes(lane, row_part, layer))) & edge_valid
+
+    def edge(half, k):
+        rows = pl.ds(EDGE_AT + k, SUB, stride=16)
+        value = jnp.where(odd == half, own_ref[rows, :], other_ref[rows, :])
+        return jnp.where(near_row, value, opposite_class(value, lane))
+
+    total = jnp.where(usable, edge(1, 10), 1.0)
+    for half, named in enumerate((LOW_ROWS, HIGH_ROWS)):
+        for k, pair in enumerate(named):
+            if pair < 21:
+                edge_ref[pair] = edge(half, k) / total
+
+    inside = inside_rows(brick, bricks, 12, 32)
+    density = jnp.where(inside, wide_ref[9, 4:36, :], 1.0)
+    fresh = velocity_update(
+        wide_ref, [wide_ref[6 + at, 4:36, :] for at in range(3)], density, inside, 32
+    )
+    for at in range(3):
+        first_velocity_ref[at] = fresh[at]
+    own_stiff = lambda pair: own_ref[pl.ds(pair, SUB, stride=24), :]
+    for group, stiff, valid in (
+        (SUB, own_stiff, None),
+        (2 * SUB - odd * 2 * SUB, lambda pair: other_ref[pl.ds(pair, SUB, stride=24), :], None),
+        (odd * 2 * SUB, lambda pair: edge_ref[pair], edge_valid),
+    ):
+        fresh = stress_update(
+            first_velocity_ref,
+            group + 4,
+            [wide_ref[at, pl.ds(group + SUB, SUB), :] for at in range(6)],
+            stiff,
+        )
+        for at in range(6):
+            value = fresh[at] if valid is None else jnp.where(valid, fresh[at], 0.0)
+            first_stress_ref[at, pl.ds(group, SUB), :] = value
+
     velocity = velocity_update(
-        wide_ref,
-        [velocity_ref[at] for at in range(3)],
-        density_ref[...],
-        inside_rows(brick, bricks),
+        first_stress_ref,
+        [first_velocity_ref[at, 8:24, :] for at in range(3)],
+        density[8:24],
+        inside_rows(brick, bricks, 4, 16),
+        16,
     )
     for at in range(3):
-        moving_ref[at] = velocity[at]
+        last_velocity_ref[at] = velocity[at]
     stress = stress_update(
-        moving_ref,
-        [stress_ref[at] for at in range(6)],
-        lambda pair: stiff_ref[pl.ds(pair, SUB, stride=24), :],
-    )
-    own = lax.axis_index("gy") * 64 + lax.axis_index("ga") * 8
+        last_velocity_ref, 4, [first_stress_ref[at, 8:16, :] for at in range(6)], own_stiff
+    )
+    own = row_part * 64 + layer * 8
 
     def put(out_ref, at, value):
         for y in range(4):
@@ -681,7 +731,7 @@
             out_ref[pl.ds(at * 32 + y, SUB, stride=4), :] = turned[:, 0:8]
 
     for at in range(3):
-        put(out_velocity_ref, at, moving_ref[at, 4:12, :])
+        put(out_velocity_ref, at, last_velocity_ref[at, 4:12, :])
     for at in range(6):
         put(out_stress_ref, at, stress[at])
 
@@ -735,41 +785,14 @@
         tiled=True,
     ).reshape(devices * BLOCK_ROWS, LANES)
     small = pltpu.CompilerParams(vmem_limit_bytes=8 * 2**20)
-    own_half = pl.pallas_call(
-        field_kernel,
-        out_shape=jax.ShapeDtypeStruct((HALF, 4 * SUB, LANES), f32),
+    own_part = pl.pallas_call(
+        unpack_kernel,
+        out_shape=jax.ShapeDtypeStruct((WIDE_AT + HALF * WIDE_ROWS, LANES), f32),
         in_specs=[vmem],
         out_specs=vmem,
         compiler_params=small,
     )(got)
-    partners = [(i, i ^ 1) for i in range(part_x)]
-    other_half = lax.ppermute(own_half, "gx", partners)
-    stiff = pl.pallas_call(
-        sums_kernel,
-        out_shape=jax.ShapeDtypeStruct((part_x * 24, LANES), f32),
-        in_specs=[vmem],
-        out_specs=vmem,
-        cost_estimate=pl.CostEstimate(flops=100000, bytes_accessed=200000, transcendentals=0),
-        compiler_params=small,
-    )(got)
-    middle_stress, middle_velocity, wide_density = pl.pallas_call(
-        functools.partial(first_step_kernel, bricks=part_x),
-        out_shape=(
-            jax.ShapeDtypeStruct((6, SUB, LANES), f32),
-            jax.ShapeDtypeStruct((3, 16, LANES), f32),
-            jax.ShapeDtypeStruct((16, LANES), f32),
-        ),
-        in_specs=[vmem] * 3,
-        out_specs=(vmem,) * 3,
-        scratch_shapes=[
-            pltpu.VMEM((FIELDS, 24, LANES), f32),
-            pltpu.VMEM((3, 16, LANES), f32),
-        ],
-        compiler_params=small,
-    )(own_half, other_half, stiff)
-    pair = lax.ppermute(middle_stress, "gx", partners)
-    swaps = [(i, i + 1) for i in range(1, part_x - 1, 2)]
-    cross = lax.ppermute(middle_stress, "gx", swaps + [(b, a) for a, b in swaps])
+    other_part = lax.ppermute(own_part, "gx", [(i, i ^ 1) for i in range(part_x)])
     stiffness = pl.pallas_call(
         stiffness_kernel,
         out_shape=jax.ShapeDtypeStruct((SUB * 4 * 8, 21), f32),
@@ -777,22 +800,25 @@
         out_specs=vmem,
         scratch_shapes=[pltpu.VMEM((LANES, 24), f32)],
         cost_estimate=pl.CostEstimate(flops=100000, bytes_accessed=200000, transcendentals=0),
-        compiler_params=pltpu.CompilerParams(vmem_limit_bytes=8 * 2**20),
-    )(stiff)
+        compiler_params=small,
+    )(own_part)
     new_velocity, new_stress = pl.pallas_call(
-        functools.partial(last_step_kernel, bricks=part_x),
+        functools.partial(steps_kernel, bricks=part_x),
         out_shape=(
             jax.ShapeDtypeStruct((3 * SUB * 4, 8), f32),
             jax.ShapeDtypeStruct((6 * SUB * 4, 8), f32),
         ),
-        in_specs=[vmem] * 6,
+        in_specs=[vmem] * 2,
         out_specs=(vmem,) * 2,
         scratch_shapes=[
-            pltpu.VMEM((6, 24, LANES), f32),
-            pltpu.VMEM((3, 16, LANES), f32),
+            pltpu.VMEM((FIELDS, 5 * SUB, LANES), f32),
+            pltpu.VMEM((21, SUB, LANES), f32),
+            pltpu.VMEM((3, 4 * SUB, LANES), f32),
+            pltpu.VMEM((6, 3 * SUB, LANES), f32),
+            pltpu.VMEM((3, 2 * SUB, LANES), f32),
         ],
-        compiler_params=pltpu.CompilerParams(vmem_limit_bytes=8 * 2**20),
-    )(middle_stress, pair, cross, middle_velocity, wide_density, stiff)
+        compiler_params=small,
+    )(own_part, other_part)
     return (
         stiffness.reshape(SUB, 4, 8, 21).transpose(3, 0, 1, 2),
         new_velocity.reshape(3, SUB, 4, 8),

time: 31.5 us -> 29.5 us (0.937)
  the two profiles are of different devices: /device:TPU:1 before, /device:TPU:0 now
where the time goes in v4:
time: 29.5 us; the launch traced here: 29.3 us
  blocking collectives  21.7 us (74%)
  Pallas kernels  6.17 us (21%)
  waiting for transfers between devices  0.69 us (2%)
  between operations  0.66 us (2%)
    all_to_all x1, blocking collectives, on_plane(): lax.all_to_all(send.reshape(devices, 1, BLOCK_ROWS * LANES), ('gx', 'gy',...  21.7 us
    pallas_call x1, Pallas kernels, on_plane(): pl.pallas_call(grain_kernel, out_shape=jax.ShapeDtypeStruct((devices * BL...  3.42 us
    pallas_call x1, Pallas kernels, on_plane(): pl.pallas_call(functools.partial(steps_kernel, bricks=part_x), out_shape=...  1.64 us
    pallas_call x1, Pallas kernels, on_plane(): pl.pallas_call(stiffness_kernel, out_shape=jax.ShapeDtypeStruct((SUB * 4...  0.87 us
    ppermute x1, waiting for transfers between devices, on_plane(): lax.ppermute(own_part, 'gx', [(i, i ^ 1) for i in range(part_x)])  0.69 us
  transfers between devices with their start and end apart: 1, of which 1 were waited for; matrix products, arithmetic and copies ran while one was open for 0% of the time, Pallas kernels for 3%

profile of v4, /device:TPU:0, one launch (start us, length us, event | category | flops | bytes accessed | tf_op | source)
XLA Modules:
  0.0 29.3 jit_solution(3869307829373230022)
XLA Ops:
  0.6 3.4 %shard_map.103 = f32[864,128]{1,0:T(8,128)S(1)} custom-call(f32[21]{0:T(128)} %crystal_hbm.1, f32[3,2048]{1,0:T(4,128)} %euler_hbm.1, s32[64,128]{1,0:T(8,128)} %bitcast.18, bf16[16,512]{1,0:T(8,128)(2,1)} %bitcast.19, s32[1,512]{1,0:T(1,128)} %bitcast.21, f32[32,8]{1,0:T(8,128)} %bitcast.20, f32[96,8]{1,0:T(8,128)} %bitcast.17, f32[192,8]{1,0:T(8,128)} %bitcast.16), custom_call_target="tpu_custom_call" | custom-call | tf_op jit(solution)/shard_map/pallas_call | solution.py:749
  4.1 21.7 %all_to_all.5 = f32[32,1,3456]{2,1,0:T(1,128)S(1)} all-to-all(f32[32,1,3456]{2,1,0:T(1,128)S(1)} %bitcast.13), channel_id=1, replica_groups=mesh['gx'=8,'gy'=2,'ga'=2] {'gx','gy','ga'}, dimensions={0} | all-to-all | bytes 884736 | tf_op jit(solution)/shard_map/all_to_all | solution.py:780
  25.8 0.2 shard_map.104.stiff_ref.own_ref
  26.0 0.1 collective-permute-start
  26.1 0.9 %shard_map.105 = f32[256,21]{1,0:T(8,128)} custom-call(f32[560,128]{1,0:T(8,128)S(1)} %shard_map.104.stiff_ref.own_ref), custom_call_target="tpu_custom_call" | custom-call | flops 100000 | bytes 200000 | tf_op jit(solution)/shard_map/pallas_call | solution.py:796
  27.0 0.7 %collective-permute-done.other_ref = f32[560,128]{1,0:T(8,128)S(1)} collective-permute-done((f32[560,128]{1,0:T(8,128)S(1)}, f32[560,128]{1,0:T(8,128)S(1)}, u32[]{:S(2)}, u32[]{:S(2)}) %collective-permute-start) | collective-permute-done | bytes 286752 | tf_op jit(solution)/shard_map/ppermute | solution.py:795
  27.7 1.6 %shard_map.106 = (f32[96,8]{1,0:T(8,128)}, f32[192,8]{1,0:T(8,128)}) custom-call(f32[560,128]{1,0:T(8,128)S(1)} %shard_map.104.stiff_ref.own_ref, f32[560,128]{1,0:T(8,128)S(1)} %collective-permute-done.other_ref), custom_call_target="tpu_custom_call" | custom-call | tf_op jit(solution)/shard_map/pallas_call | solution.py:805
Async XLA Ops:
  26.0 1.6 %collective-permute-start = (f32[560,128]{1,0:T(8,128)S(1)}, f32[560,128]{1,0:T(8,128)S(1)}, u32[]{:S(2)}, u32[]{:S(2)}) collective-permute-start(f32[560,128]{1,0:T(8,128)S(1)} %shard_map.104.stiff_ref.own_ref), channel_id=1, source_target_pairs={{0,4},{4,0},{8,12},{12,8},{16,20},{20,16},{24,28},{28,24},{1,5},{5... | collective-permute-start | bytes 860168 | tf_op jit(solution)/shard_map/ppermute | solution.py:795

commit v5 on v4

--- a/solution.py
+++ b/solution.py
@@ -247,7 +247,8 @@
         and brick_z == 8
         and orient.shape[3] == part_x * 64
         and orient.shape[0] % 8 == 0
-        and euler_table.shape[1] % LANES == 0
+        and euler_table.shape[1] in [LANES << level for level in range(8)]
+        and STEPS == 2
     )
 
 
@@ -270,37 +271,137 @@
     return (lane // 64 == row_half) | ((lane // 8) % 2 == layer)
 
 
-def bond_matrix(trig):
+def cos_and_sin(angle):
+    turns = jnp.floor(angle * 0.6366197723675814 + 0.5)
+    rest = angle - turns * 1.5703125
+    rest = rest - turns * 4.837512969970703e-4
+    rest = rest - turns * 7.549789948768648e-8
+    square = rest * rest
+    sin_poly = (-1.9515295891e-4 * square + 8.3321608736e-3) * square - 1.6666654611e-1
+    sin = rest + rest * square * sin_poly
+    cos_poly = (2.443315711809948e-5 * square - 1.388731625493765e-3) * square
+    cos = 1.0 - 0.5 * square + square * square * (cos_poly + 4.166664568298827e-2)
+    quarter = turns.astype(jnp.int32)
+    odd = (quarter & 1) == 1
+    turned_cos, turned_sin = jnp.where(odd, sin, cos), jnp.where(odd, cos, sin)
+    return (
+        jnp.where(((quarter + 1) & 2) == 2, -turned_cos, turned_cos),
+        jnp.where((quarter & 2) == 2, -turned_sin, turned_sin),
+    )
+
+
+def multiples(c, s):
+    c2 = 2.0 * (c * c) - 1.0
+    s2 = 2.0 * (c * s)
+    return (
+        (c, s),
+        (c2, s2),
+        (c2 * c - s2 * s, s2 * c + c2 * s),
+        (2.0 * (c2 * c2) - 1.0, 2.0 * (c2 * s2)),
+    )
+
+
+def adapted(entries, axes):
+    one, two, three, shear, first, second = axes
+    at = lambda row, col: entries[(min(row, col), max(row, col))]
+    mean = at(one, one) + at(two, two)
+    cross = 2.0 * at(one, two)
+    spread = mean - cross
+    half_shear = 0.5 * at(shear, shear)
+    half_spread = 0.5 * spread
+    half_first = 0.5 * at(first, first)
+    half_second = 0.5 * at(second, second)
+    lone = lambda with_: (at(one, with_) + at(two, with_), at(one, with_) - at(two, with_))
+    sum_three, diff_three = lone(three)
+    sum_shear, diff_shear = lone(shear)
+    sum_first, diff_first = lone(first)
+    sum_second, diff_second = lone(second)
+    fixed = (
+        mean + cross,
+        sum_three,
+        at(three, three),
+        half_spread + half_shear,
+        half_first + half_second,
+    )
+    pairs = [
+        (2, at(one, one) - at(two, two), sum_shear),
+        (2, diff_three, at(three, shear)),
+        (1, sum_first, sum_second),
+        (1, at(three, first), at(three, second)),
+        (4, half_spread - half_shear, diff_shear),
+        (2, half_first - half_second, at(first, second)),
+        (1, diff_first + at(shear, second), at(shear, first) - diff_second),
+        (3, diff_first - at(shear, second), at(shear, first) + diff_second),
+    ]
+    return fixed, pairs
+
+
+def turned(adapted_set, angles):
+    fixed, pairs = adapted_set
+    fresh = []
+    for order, x, y in pairs:
+        c, s = angles[order - 1]
+        fresh.append((order, c * x - s * y, s * x + c * y))
+    return fixed, fresh
+
+
+def natural(adapted_set, axes):
+    one, two, three, shear, first, second = axes
+    (whole, sum_three, three_three, shear_mean, side_mean), pairs = adapted_set
+    (
+        (_, lean, sum_shear),
+        (_, diff_three, three_shear),
+        (_, sum_first, sum_second),
+        (_, three_first, three_second),
+        (_, shear_half, diff_shear),
+        (_, side_half, first_second),
+        (_, real_one, imag_one),
+        (_, real_three, imag_three),
+    ) = pairs
+    spread = shear_mean + shear_half
+    diff_first = 0.5 * (real_one + real_three)
+    diff_second = 0.5 * (imag_three - imag_one)
+    quarter = 0.25 * (whole + spread)
+    half_lean = 0.5 * lean
+    out = {}
+
+    def put(row, col, value):
+        out[(min(row, col), max(row, col))] = value
+
+    put(one, one, quarter + half_lean)
+    put(two, two, quarter - half_lean)
+    put(one, two, 0.25 * (whole - spread))
+    for with_, total, gap in (
+        (three, sum_three, diff_three),
+        (shear, sum_shear, diff_shear),
+        (first, sum_first, diff_first),
+        (second, sum_second, diff_second),
+    ):
+        put(one, with_, 0.5 * (total + gap))
+        put(two, with_, 0.5 * (total - gap))
+    put(three, three, three_three)
+    put(three, shear, three_shear)
+    put(three, first, three_first)
+    put(three, second, three_second)
+    put(shear, shear, shear_mean - shear_half)
+    put(shear, first, 0.5 * (imag_one + imag_three))
+    put(shear, second, 0.5 * (real_one - real_three))
+    put(first, first, side_mean + side_half)
+    put(second, second, side_mean - side_half)
+    put(first, second, first_second)
+    return out
+
+
+about_z = (0, 1, 2, 5, 4, 3)
+about_x = (1, 2, 0, 3, 5, 4)
+
+
+def rotated_stiffness(entries, trig):
     cos_one, cos_mid, cos_two, sin_one, sin_mid, sin_two = trig
-    cos_two_mid = cos_two * cos_mid
-    sin_two_mid = sin_two * cos_mid
-    bunge = [
-        [
-            cos_one * cos_two - sin_one * sin_two_mid,
-            sin_one * cos_two + cos_one * sin_two_mid,
-            sin_two * sin_mid,
-        ],
-        [
-            -cos_one * sin_two - sin_one * cos_two_mid,
-            -sin_one * sin_two + cos_one * cos_two_mid,
-            cos_two * sin_mid,
-        ],
-        [sin_one * sin_mid, -cos_one * sin_mid, cos_mid],
-    ]
-    rotation = [[bunge[col][row] for col in range(3)] for row in range(3)]
-    bond = []
-    for first, second in voigt_pairs:
-        row = []
-        for in_index, (third, fourth) in enumerate(voigt_pairs):
-            if in_index < 3:
-                row.append(rotation[first][third] * rotation[second][third])
-            else:
-                row.append(
-                    rotation[first][third] * rotation[second][fourth]
-                    + rotation[first][fourth] * rotation[second][third]
-                )
-        bond.append(row)
-    return bond
+    first = turned(adapted(entries, about_z), multiples(cos_two, sin_two))
+    middle = turned(adapted(natural(first, about_z), about_x), multiples(cos_mid, sin_mid))
+    last = turned(adapted(natural(middle, about_x), about_z), multiples(cos_one, sin_one))
+    return natural(last, about_z)
 
 
 def grain_kernel(
@@ -325,6 +426,7 @@
     sums_ref,
     place_ref,
     acc_ref,
+    fields_ref,
     arrived,
 ):
     row_part = lax.axis_index("gy")
@@ -357,15 +459,15 @@
     place_ref[...] = jnp.zeros_like(place_ref)
 
     copies[0].wait()
-    angles = euler_ref[...]
-    trig_ref[0:3, :] = jnp.cos(angles)
-    trig_ref[3:6, :] = jnp.sin(angles)
-
-    for copy in copies[1:4]:
+    trig_ref[0:3, :], trig_ref[3:6, :] = cos_and_sin(euler_ref[...])
+
+    for copy in copies[1:]:
         copy.wait()
-    entries = [
-        [crystal_ref[symmetric_index(row, col)] for col in range(6)] for row in range(6)
-    ]
+    scale = (1.0, 1.0, 1.0, 2.0, 2.0, 2.0)
+    entries = {
+        (row, col): (scale[row] * scale[col]) * crystal_ref[pair]
+        for pair, (row, col) in enumerate(upper_pairs)
+    }
     row_of = {}
     for k in range(len(LOW_ROWS)):
         row_of[LOW_ROWS[k]] = k
@@ -373,66 +475,31 @@
 
     def pick(tile, octet):
         index = orient_ref[pl.ds(octet * SUB * tiles + tile, SUB, stride=tiles), :]
-        low, high = index & (LANES - 1), index >> 7
-        values = [None] * 6
-        for table_tile in range(table_tiles):
-            here = high == table_tile
-            for which in range(6):
+        low = index & (LANES - 1)
+        bits = [(index & (LANES << level)) != 0 for level in range(table_tiles.bit_length() - 1)]
+
+        def find(which, first, level):
+            if level == 0:
                 source = jnp.broadcast_to(
-                    trig_ref[
-                        which : which + 1, table_tile * LANES : (table_tile + 1) * LANES
-                    ],
-                    (SUB, LANES),
+                    trig_ref[which : which + 1, first * LANES : (first + 1) * LANES], (SUB, LANES)
                 )
-                found = jnp.take_along_axis(source, low, axis=1, mode="promise_in_bounds")
-                values[which] = found if table_tile == 0 else jnp.where(here, found, values[which])
+                return jnp.take_along_axis(source, low, axis=1, mode="promise_in_bounds")
+            lower = find(which, first, level - 1)
+            upper = find(which, first + (1 << (level - 1)), level - 1)
+            return jnp.where(bits[level - 1], upper, lower)
+
+        values = [find(which, 0, len(bits)) for which in range(6)]
         return values
 
-    def one_tile(tile, unused):
-        for octet in range(octets):
-            bond = bond_matrix(pick(tile, octet))
-            mass = weight_ref[
-                octet * SUB : (octet + 1) * SUB, pl.ds(pl.multiple_of(tile * LANES, LANES), LANES)
-            ].astype(jnp.float32)
-            pair = 0
-            for row in range(6):
-                product = [
-                    ordered_sum([bond[row][inner] * entries[inner][col] for inner in range(6)])
-                    * mass
-                    for col in range(6)
-                ]
-                for col in range(row, 6):
-                    value = ordered_sum([product[inner] * bond[col][inner] for inner in range(6)])
-                    acc_ref[pair] = value if octet == 0 else acc_ref[pair] + value
-                    pair += 1
-            acc_ref[21] = mass if octet == 0 else acc_ref[21] + mass
-        for pair in range(22):
-            sums_ref[
-                row_of[pair] : row_of[pair] + 1, pl.ds(pl.multiple_of(tile * LANES, LANES), LANES)
-            ] = jnp.sum(acc_ref[pair], axis=0, keepdims=True)
-        return unused
-
-    lax.fori_loop(0, tiles, one_tile, 0)
-    for copy in copies[4:]:
-        copy.wait()
+    held = [pick(0, octet) for octet in range(octets)]
 
     slots = map_ref[...]
-    half = cells // (cells // 32)
+    half = 32
     for chunk in range(cells // half):
         wanted = rows_of((half, cells)) + chunk * half
         hit = jnp.where(jnp.broadcast_to(slots, (half, cells)) == wanted, 1.0, 0.0)
         start = pl.multiple_of(chunk * 2 * half + row_part * half, half)
         place_ref[pl.ds(start, half), :] = hit.astype(jnp.bfloat16)
-    sums = sums_ref[...]
-    part_one = sums.astype(jnp.bfloat16)
-    rest = sums - part_one.astype(jnp.float32)
-    part_two = rest.astype(jnp.bfloat16)
-    part_three = (rest - part_two.astype(jnp.float32)).astype(jnp.bfloat16)
-    parts = jnp.concatenate([part_one, part_two, part_three], axis=0)
-    placed = lax.dot_general(
-        parts, place_ref[...], (((1,), (1,)), ((), ())), preferred_element_type=jnp.float32
-    )
-    placed = placed[0:32] + placed[32:64] + placed[64:96]
 
     own = row_part * 2 + layer
 
@@ -454,15 +521,48 @@
         return into
 
     nothing = jnp.zeros((SUB, LANES), jnp.float32)
-    groups, tails = [], []
     for half in range(2):
         group, tail = nothing, nothing
         for slot in range(4):
             group = spread(half * HALF + slot, slot, group)
             piece = spread(half * HALF + 4, slot, nothing)
             tail = tail + (piece if slot == 0 else pltpu.roll(piece, SUB - 2 * slot, 0))
-        groups.append(group)
-        tails.append(tail[0:2])
+        fields_ref[half, 0:SUB, :] = group
+        fields_ref[half, SUB : SUB + 2, :] = tail[0:2]
+
+    def add_tile(tile, held):
+        lanes = slice(tile * LANES, (tile + 1) * LANES)
+        for octet in range(octets):
+            rotated = rotated_stiffness(entries, held[octet])
+            mass = weight_ref[octet * SUB : (octet + 1) * SUB, lanes].astype(jnp.float32)
+            masses = {1.0: mass, 0.5: 0.5 * mass, 0.25: 0.25 * mass}
+            for pair, (row, col) in enumerate(upper_pairs):
+                value = rotated[row, col] * masses[1.0 / (scale[row] * scale[col])]
+                acc_ref[pair] = value if octet == 0 else acc_ref[pair] + value
+            acc_ref[21] = mass if octet == 0 else acc_ref[21] + mass
+        for pair in range(22):
+            at = row_of[pair]
+            sums_ref[at : at + 1, lanes] = jnp.sum(acc_ref[pair], axis=0, keepdims=True)
+
+    def one_tile(tile, held):
+        fresh = [pick(tile + 1, octet) for octet in range(octets)]
+        add_tile(tile, held)
+        return fresh
+
+    for tile in range(tiles - 1):
+        held = one_tile(tile, held)
+    add_tile(tiles - 1, held)
+
+    sums = sums_ref[...]
+    part_one = sums.astype(jnp.bfloat16)
+    rest = sums - part_one.astype(jnp.float32)
+    part_two = rest.astype(jnp.bfloat16)
+    part_three = (rest - part_two.astype(jnp.float32)).astype(jnp.bfloat16)
+    parts = jnp.concatenate([part_one, part_two, part_three], axis=0)
+    placed = lax.dot_general(
+        parts, place_ref[...], (((1,), (1,)), ((), ())), preferred_element_type=jnp.float32
+    )
+    placed = placed[0:32] + placed[32:64] + placed[64:96]
 
     shift = 32 + row_part * 64
     bricks = destinations // 4
@@ -492,24 +592,25 @@
             edge = jnp.where(near_lanes(lane, inner // 2, inner % 2), near, far)
             send_ref[at : at + SUM_ROWS, :] = own_sums[brick][0:SUM_ROWS]
             send_ref[at + SUM_ROWS : at + FIELD_AT, :] = edge[0:EDGE_ROWS]
-            send_ref[at + FIELD_AT : at + FIELD_AT + SUB, :] = groups[side]
-            send_ref[at + FIELD_AT + SUB : at + BLOCK_ROWS, :] = tails[side]
-
-
-def plane_derivative(field, dim, lane):
-    position = lane // 16 if dim == 1 else lane % 16
-    extent = 8 if dim == 1 else 16
-    unit = 16 if dim == 1 else 1
-    total = None
+            send_ref[at + FIELD_AT : at + FIELD_AT + SUB, :] = fields_ref[side, 0:SUB, :]
+            send_ref[at + FIELD_AT + SUB : at + BLOCK_ROWS, :] = fields_ref[side, SUB : SUB + 2, :]
+
+
+def plane_shifts(dim, count):
+    lane = lanes_of((count, LANES))
+    position, extent, unit = (lane // 16, 8, 16) if dim == 1 else (lane % 16, 16, 1)
+    terms = {}
     for order in range(1, 5):
-        ahead = pltpu.roll(field, LANES - order * unit, 1)
-        behind = pltpu.roll(field, order * unit, 1)
-        term = stencil_weights[order - 1] * (
-            jnp.where(position + order < extent, ahead, 0.0)
-            - jnp.where(position - order >= 0, behind, 0.0)
-        )
-        total = term if total is None else total + term
-    return total
+        weight = stencil_weights[order - 1]
+        behind = jnp.where(position >= order, -weight, 0.0)
+        ahead = jnp.where(position < extent - order, weight, 0.0)
+        for shift, own in ((order * unit, behind), (LANES - order * unit, ahead)):
+            terms[shift] = terms[shift] + own if shift in terms else own
+    return list(terms.items())
+
+
+def plane_derivative(field, shifts):
+    return ordered_sum([weights * pltpu.roll(field, shift, 1) for shift, weights in shifts])
 
 
 def row_derivative(read, start, count):
@@ -522,14 +623,14 @@
 
 
 def velocity_update(wide_stress, old_velocity, density, inside, count):
-    lane = lanes_of((count, LANES))
+    shifts = {dim: plane_shifts(dim, count) for dim in (1, 2)}
 
     def along(component, dim):
         if dim == 0:
             return row_derivative(
                 lambda at, size: wide_stress[component, at : at + size, :], 4, count
             )
-        return plane_derivative(wide_stress[component, 4 : 4 + count, :], dim, lane)
+        return plane_derivative(wide_stress[component, 4 : 4 + count, :], shifts[dim])
 
     sums = [
         along(0, 0) + along(5, 1) + along(4, 2),
@@ -543,14 +644,14 @@
 
 
 def stress_update(wide_velocity, start, old_stress, stiff):
-    lane = lanes_of((SUB, LANES))
+    shifts = {dim: plane_shifts(dim, SUB) for dim in (1, 2)}
 
     def along(component, dim):
         if dim == 0:
             return row_derivative(
                 lambda at, size: wide_velocity[component, pl.ds(at, size), :], start, SUB
             )
-        return plane_derivative(wide_velocity[component, pl.ds(start, SUB), :], dim, lane)
+        return plane_derivative(wide_velocity[component, pl.ds(start, SUB), :], shifts[dim])
 
     strain = [
         along(0, 0),
@@ -764,6 +865,7 @@
             pltpu.VMEM((32, cells), f32),
             pltpu.VMEM((2 * cells, cells), jnp.bfloat16),
             pltpu.VMEM((22, SUB, LANES), f32),
+            pltpu.VMEM((2, 2 * SUB, LANES), f32),
             pltpu.SemaphoreType.DMA((8,)),
         ],
         compiler_params=pltpu.CompilerParams(vmem_limit_bytes=8 * 2**20),

time: 29.5 us -> 28.9 us (0.980)
  Pallas kernels: 6.17 us -> 5.52 us
    pallas_call x1, Pallas kernels: 3.42 us -> 2.78 us  [on_plane(): pl.pallas_call(grain_kernel, out_shape=jax.ShapeDtypeStruct((devices * BL...]
where the time goes in v5:
time: 28.9 us; the launch traced here: 28.7 us
  blocking collectives  21.7 us (75%)
  Pallas kernels  5.52 us (19%)
  waiting for transfers between devices  0.69 us (2%)
  between operations  0.66 us (2%)
    all_to_all x1, blocking collectives, on_plane(): lax.all_to_all(send.reshape(devices, 1, BLOCK_ROWS * LANES), ('gx', 'gy',...  21.7 us
    pallas_call x1, Pallas kernels, on_plane(): pl.pallas_call(grain_kernel, out_shape=jax.ShapeDtypeStruct((devices * BL...  2.78 us
    pallas_call x1, Pallas kernels, on_plane(): pl.pallas_call(functools.partial(steps_kernel, bricks=part_x), out_shape=...  1.63 us
    pallas_call x1, Pallas kernels, on_plane(): pl.pallas_call(stiffness_kernel, out_shape=jax.ShapeDtypeStruct((SUB * 4...  0.87 us
    ppermute x1, waiting for transfers between devices, on_plane(): lax.ppermute(own_part, 'gx', [(i, i ^ 1) for i in range(part_x)])  0.69 us
  transfers between devices with their start and end apart: 1, of which 1 were waited for; matrix products, arithmetic and copies ran while one was open for 0% of the time, Pallas kernels for 3%

profile of v5, /device:TPU:0, one launch (start us, length us, event | category | flops | bytes accessed | tf_op | source)
XLA Modules:
  0.0 28.7 jit_solution(7772110753101476802)
XLA Ops:
  0.6 2.8 %shard_map.103 = f32[864,128]{1,0:T(8,128)S(1)} custom-call(f32[21]{0:T(128)} %crystal_hbm.1, f32[3,2048]{1,0:T(4,128)} %euler_hbm.1, s32[64,128]{1,0:T(8,128)} %bitcast.18, bf16[16,512]{1,0:T(8,128)(2,1)} %bitcast.19, s32[1,512]{1,0:T(1,128)} %bitcast.21, f32[32,8]{1,0:T(8,128)} %bitcast.20, f32[96,8]{1,0:T(8,128)} %bitcast.17, f32[192,8]{1,0:T(8,128)} %bitcast.16), custom_call_target="tpu_custom_call" | custom-call | tf_op jit(solution)/shard_map/pallas_call | solution.py:850
  3.4 21.7 %all_to_all.5 = f32[32,1,3456]{2,1,0:T(1,128)S(1)} all-to-all(f32[32,1,3456]{2,1,0:T(1,128)S(1)} %bitcast.13), channel_id=1, replica_groups=mesh['gx'=8,'gy'=2,'ga'=2] {'gx','gy','ga'}, dimensions={0} | all-to-all | bytes 884736 | tf_op jit(solution)/shard_map/all_to_all | solution.py:882
  25.2 0.2 shard_map.104.stiff_ref.own_ref
  25.4 0.1 collective-permute-start
  25.5 0.9 %shard_map.105 = f32[256,21]{1,0:T(8,128)} custom-call(f32[560,128]{1,0:T(8,128)S(1)} %shard_map.104.stiff_ref.own_ref), custom_call_target="tpu_custom_call" | custom-call | flops 100000 | bytes 200000 | tf_op jit(solution)/shard_map/pallas_call | solution.py:898
  26.4 0.7 %collective-permute-done.other_ref = f32[560,128]{1,0:T(8,128)S(1)} collective-permute-done((f32[560,128]{1,0:T(8,128)S(1)}, f32[560,128]{1,0:T(8,128)S(1)}, u32[]{:S(2)}, u32[]{:S(2)}) %collective-permute-start) | collective-permute-done | bytes 286752 | tf_op jit(solution)/shard_map/ppermute | solution.py:897
  27.0 1.6 %shard_map.106 = (f32[96,8]{1,0:T(8,128)}, f32[192,8]{1,0:T(8,128)}) custom-call(f32[560,128]{1,0:T(8,128)S(1)} %shard_map.104.stiff_ref.own_ref, f32[560,128]{1,0:T(8,128)S(1)} %collective-permute-done.other_ref), custom_call_target="tpu_custom_call" | custom-call | tf_op jit(solution)/shard_map/pallas_call | solution.py:907
Async XLA Ops:
  25.4 1.6 %collective-permute-start = (f32[560,128]{1,0:T(8,128)S(1)}, f32[560,128]{1,0:T(8,128)S(1)}, u32[]{:S(2)}, u32[]{:S(2)}) collective-permute-start(f32[560,128]{1,0:T(8,128)S(1)} %shard_map.104.stiff_ref.own_ref), channel_id=1, source_target_pairs={{0,4},{4,0},{8,12},{12,8},{16,20},{20,16},{24,28},{28,24},{1,5},{5... | collective-permute-start | bytes 860168 | tf_op jit(solution)/shard_map/ppermute | solution.py:897

commit v6 on v5

--- a/solution.py
+++ b/solution.py
@@ -260,11 +260,32 @@
     return lax.broadcasted_iota(jnp.int32, shape, len(shape) - 2)
 
 
+def other_layer(value, lane):
+    return jnp.where(
+        (lane // 8) % 2 == 0, pltpu.roll(value, LANES - 8, 1), pltpu.roll(value, 8, 1)
+    )
+
+
 def opposite_class(value, lane):
-    value = jnp.where(
-        (lane // 8) % 2 == 0, pltpu.roll(value, LANES - 8, 1), pltpu.roll(value, 8, 1)
-    )
-    return pltpu.roll(value, LANES // 2, 1)
+    return pltpu.roll(other_layer(value, lane), LANES // 2, 1)
+
+
+def sublane_sums(values):
+    row = rows_of((SUB, LANES))
+    values = values + [None] * (SUB - len(values))
+    for step in (1, 2, 4):
+        keep = (row // step) % 2 == 0
+        merged = []
+        for one, two in zip(values[0::2], values[1::2]):
+            if one is None:
+                merged.append(None)
+                continue
+            two = jnp.zeros_like(one) if two is None else two
+            merged.append(
+                jnp.where(keep, one, two) + pltpu.roll(jnp.where(keep, two, one), step, 0)
+            )
+        values = merged
+    return values[0]
 
 
 def near_lanes(lane, row_half, layer):
@@ -422,7 +443,6 @@
     density_ref,
     velocity_ref,
     stress_ref,
-    trig_ref,
     sums_ref,
     place_ref,
     acc_ref,
@@ -442,11 +462,11 @@
         pltpu.make_async_copy(source, target, arrived.at[at])
         for at, (source, target) in enumerate(
             [
+                (orient_hbm, orient_ref),
                 (euler_hbm, euler_ref),
-                (orient_hbm, orient_ref),
+                (map_hbm, map_ref),
+                (crystal_hbm, crystal_ref),
                 (weight_hbm, weight_ref),
-                (crystal_hbm, crystal_ref),
-                (map_hbm, map_ref),
                 (stress_hbm, stress_ref),
                 (velocity_hbm, velocity_ref),
                 (density_hbm, density_ref),
@@ -458,21 +478,13 @@
     sums_ref[...] = jnp.zeros_like(sums_ref)
     place_ref[...] = jnp.zeros_like(place_ref)
 
-    copies[0].wait()
-    trig_ref[0:3, :], trig_ref[3:6, :] = cos_and_sin(euler_ref[...])
-
-    for copy in copies[1:]:
+    for copy in copies[:5]:
         copy.wait()
     scale = (1.0, 1.0, 1.0, 2.0, 2.0, 2.0)
     entries = {
         (row, col): (scale[row] * scale[col]) * crystal_ref[pair]
         for pair, (row, col) in enumerate(upper_pairs)
     }
-    row_of = {}
-    for k in range(len(LOW_ROWS)):
-        row_of[LOW_ROWS[k]] = k
-        row_of[HIGH_ROWS[k]] = 16 + k
-
     def pick(tile, octet):
         index = orient_ref[pl.ds(octet * SUB * tiles + tile, SUB, stride=tiles), :]
         low = index & (LANES - 1)
@@ -481,14 +493,14 @@
         def find(which, first, level):
             if level == 0:
                 source = jnp.broadcast_to(
-                    trig_ref[which : which + 1, first * LANES : (first + 1) * LANES], (SUB, LANES)
+                    euler_ref[which : which + 1, first * LANES : (first + 1) * LANES], (SUB, LANES)
                 )
                 return jnp.take_along_axis(source, low, axis=1, mode="promise_in_bounds")
             lower = find(which, first, level - 1)
             upper = find(which, first + (1 << (level - 1)), level - 1)
             return jnp.where(bits[level - 1], upper, lower)
 
-        values = [find(which, 0, len(bits)) for which in range(6)]
+        values = [find(which, 0, len(bits)) for which in range(3)]
         return values
 
     held = [pick(0, octet) for octet in range(octets)]
@@ -501,6 +513,32 @@
         start = pl.multiple_of(chunk * 2 * half + row_part * half, half)
         place_ref[pl.ds(start, half), :] = hit.astype(jnp.bfloat16)
 
+    def add_tile(tile, held):
+        lanes = slice(tile * LANES, (tile + 1) * LANES)
+        for octet in range(octets):
+            turns = [cos_and_sin(angle) for angle in held[octet]]
+            rotated = rotated_stiffness(entries, [turn[at] for at in range(2) for turn in turns])
+            mass = weight_ref[octet * SUB : (octet + 1) * SUB, lanes].astype(jnp.float32)
+            masses = {1.0: mass, 0.5: 0.5 * mass, 0.25: 0.25 * mass}
+            for pair, (row, col) in enumerate(upper_pairs):
+                value = rotated[row, col] * masses[1.0 / (scale[row] * scale[col])]
+                acc_ref[pair] = value if octet == 0 else acc_ref[pair] + value
+            acc_ref[21] = mass if octet == 0 else acc_ref[21] + mass
+        for at, named in enumerate((LOW_ROWS, HIGH_ROWS)):
+            for first in (0, SUB):
+                summed = sublane_sums([acc_ref[pair] for pair in named[first : first + SUB]])
+                sums_ref[at * 16 + first : at * 16 + first + SUB, lanes] = summed
+
+    def one_tile(tile, held):
+        fresh = [pick(tile + 1, octet) for octet in range(octets)]
+        add_tile(tile, held)
+        return fresh
+
+    for tile in range(tiles // 2):
+        held = one_tile(tile, held)
+
+    for copy in copies[5:]:
+        copy.wait()
     own = row_part * 2 + layer
 
     def field_rows(component, y):
@@ -523,33 +561,19 @@
     nothing = jnp.zeros((SUB, LANES), jnp.float32)
     for half in range(2):
         group, tail = nothing, nothing
-        for slot in range(4):
+        for slot in (0, 1, 3, 2):
             group = spread(half * HALF + slot, slot, group)
-            piece = spread(half * HALF + 4, slot, nothing)
+            if slot == 0:
+                piece = spread(half * HALF + 4, slot, nothing)
+            elif slot == 3:
+                piece = pltpu.roll(piece, LANES // 2, 1)
+            else:
+                piece = other_layer(piece, lanes_of((SUB, LANES)))
             tail = tail + (piece if slot == 0 else pltpu.roll(piece, SUB - 2 * slot, 0))
         fields_ref[half, 0:SUB, :] = group
         fields_ref[half, SUB : SUB + 2, :] = tail[0:2]
 
-    def add_tile(tile, held):
-        lanes = slice(tile * LANES, (tile + 1) * LANES)
-        for octet in range(octets):
-            rotated = rotated_stiffness(entries, held[octet])
-            mass = weight_ref[octet * SUB : (octet + 1) * SUB, lanes].astype(jnp.float32)
-            masses = {1.0: mass, 0.5: 0.5 * mass, 0.25: 0.25 * mass}
-            for pair, (row, col) in enumerate(upper_pairs):
-                value = rotated[row, col] * masses[1.0 / (scale[row] * scale[col])]
-                acc_ref[pair] = value if octet == 0 else acc_ref[pair] + value
-            acc_ref[21] = mass if octet == 0 else acc_ref[21] + mass
-        for pair in range(22):
-            at = row_of[pair]
-            sums_ref[at : at + 1, lanes] = jnp.sum(acc_ref[pair], axis=0, keepdims=True)
-
-    def one_tile(tile, held):
-        fresh = [pick(tile + 1, octet) for octet in range(octets)]
-        add_tile(tile, held)
-        return fresh
-
-    for tile in range(tiles - 1):
+    for tile in range(tiles // 2, tiles - 1):
         held = one_tile(tile, held)
     add_tile(tiles - 1, held)
 
@@ -861,7 +885,6 @@
             pltpu.VMEM((SUB * 4, 8), f32),
             pltpu.VMEM((3 * SUB * 4, 8), f32),
             pltpu.VMEM((6 * SUB * 4, 8), f32),
-            pltpu.VMEM((SUB, euler_table.shape[1]), f32),
             pltpu.VMEM((32, cells), f32),
             pltpu.VMEM((2 * cells, cells), jnp.bfloat16),
             pltpu.VMEM((22, SUB, LANES), f32),

time: 28.9 us -> 28.5 us (0.986)
  Pallas kernels: 5.52 us -> 5.15 us
    pallas_call x1, Pallas kernels: 2.78 us -> 2.41 us  [on_plane(): pl.pallas_call(grain_kernel, out_shape=jax.ShapeDtypeStruct((devices * BL...]
where the time goes in v6:
time: 28.5 us; the launch traced here: 28.3 us
  blocking collectives  21.7 us (76%)
  Pallas kernels  5.15 us (18%)
  waiting for transfers between devices  0.69 us (2%)
  between operations  0.66 us (2%)
    all_to_all x1, blocking collectives, on_plane(): lax.all_to_all(send.reshape(devices, 1, BLOCK_ROWS * LANES), ('gx', 'gy',...  21.7 us
    pallas_call x1, Pallas kernels, on_plane(): pl.pallas_call(grain_kernel, out_shape=jax.ShapeDtypeStruct((devices * BL...  2.41 us
    pallas_call x1, Pallas kernels, on_plane(): pl.pallas_call(functools.partial(steps_kernel, bricks=part_x), out_shape=...  1.63 us
    pallas_call x1, Pallas kernels, on_plane(): pl.pallas_call(stiffness_kernel, out_shape=jax.ShapeDtypeStruct((SUB * 4...  0.87 us
    ppermute x1, waiting for transfers between devices, on_plane(): lax.ppermute(own_part, 'gx', [(i, i ^ 1) for i in range(part_x)])  0.69 us
  transfers between devices with their start and end apart: 1, of which 1 were waited for; matrix products, arithmetic and copies ran while one was open for 0% of the time, Pallas kernels for 3%

profile of v6, /device:TPU:0, one launch (start us, length us, event | category | flops | bytes accessed | tf_op | source)
XLA Modules:
  0.0 28.3 jit_solution(3388521372815852325)
XLA Ops:
  0.6 2.4 %shard_map.103 = f32[864,128]{1,0:T(8,128)S(1)} custom-call(f32[21]{0:T(128)} %crystal_hbm.1, f32[3,2048]{1,0:T(4,128)} %euler_hbm.1, s32[64,128]{1,0:T(8,128)} %bitcast.18, bf16[16,512]{1,0:T(8,128)(2,1)} %bitcast.19, s32[1,512]{1,0:T(1,128)} %bitcast.21, f32[32,8]{1,0:T(8,128)} %bitcast.20, f32[96,8]{1,0:T(8,128)} %bitcast.17, f32[192,8]{1,0:T(8,128)} %bitcast.16), custom_call_target="tpu_custom_call" | custom-call | tf_op jit(solution)/shard_map/pallas_call | solution.py:874
  3.1 21.7 %all_to_all.5 = f32[32,1,3456]{2,1,0:T(1,128)S(1)} all-to-all(f32[32,1,3456]{2,1,0:T(1,128)S(1)} %bitcast.13), channel_id=1, replica_groups=mesh['gx'=8,'gy'=2,'ga'=2] {'gx','gy','ga'}, dimensions={0} | all-to-all | bytes 884736 | tf_op jit(solution)/shard_map/all_to_all | solution.py:905
  24.8 0.2 shard_map.104.stiff_ref.own_ref
  25.0 0.1 collective-permute-start
  25.1 0.9 %shard_map.105 = f32[256,21]{1,0:T(8,128)} custom-call(f32[560,128]{1,0:T(8,128)S(1)} %shard_map.104.stiff_ref.own_ref), custom_call_target="tpu_custom_call" | custom-call | flops 100000 | bytes 200000 | tf_op jit(solution)/shard_map/pallas_call | solution.py:921
  26.0 0.7 %collective-permute-done.other_ref = f32[560,128]{1,0:T(8,128)S(1)} collective-permute-done((f32[560,128]{1,0:T(8,128)S(1)}, f32[560,128]{1,0:T(8,128)S(1)}, u32[]{:S(2)}, u32[]{:S(2)}) %collective-permute-start) | collective-permute-done | bytes 286752 | tf_op jit(solution)/shard_map/ppermute | solution.py:920
  26.7 1.6 %shard_map.106 = (f32[96,8]{1,0:T(8,128)}, f32[192,8]{1,0:T(8,128)}) custom-call(f32[560,128]{1,0:T(8,128)S(1)} %shard_map.104.stiff_ref.own_ref, f32[560,128]{1,0:T(8,128)S(1)} %collective-permute-done.other_ref), custom_call_target="tpu_custom_call" | custom-call | tf_op jit(solution)/shard_map/pallas_call | solution.py:930
Async XLA Ops:
  25.0 1.6 %collective-permute-start = (f32[560,128]{1,0:T(8,128)S(1)}, f32[560,128]{1,0:T(8,128)S(1)}, u32[]{:S(2)}, u32[]{:S(2)}) collective-permute-start(f32[560,128]{1,0:T(8,128)S(1)} %shard_map.104.stiff_ref.own_ref), channel_id=1, source_target_pairs={{0,4},{4,0},{8,12},{12,8},{16,20},{20,16},{24,28},{28,24},{1,5},{5... | collective-permute-start | bytes 860168 | tf_op jit(solution)/shard_map/ppermute | solution.py:920

commit v7 on v6

--- a/solution.py
+++ b/solution.py
@@ -286,6 +286,10 @@
             )
         values = merged
     return values[0]
+
+
+def block_of(brick, inner, bricks):
+    return (inner % 2) * bricks * 2 + brick * 2 + inner // 2
 
 
 def near_lanes(lane, row_half, layer):
@@ -507,11 +511,15 @@
 
     slots = map_ref[...]
     half = 32
+    inner = jnp.where(
+        jnp.broadcast_to(slots & (half - 1), (half, cells)) == rows_of((half, cells)), 1.0, 0.0
+    ).astype(jnp.bfloat16)
+    outer = jnp.broadcast_to(slots // half, (half, cells)).astype(jnp.bfloat16)
     for chunk in range(cells // half):
-        wanted = rows_of((half, cells)) + chunk * half
-        hit = jnp.where(jnp.broadcast_to(slots, (half, cells)) == wanted, 1.0, 0.0)
         start = pl.multiple_of(chunk * 2 * half + row_part * half, half)
-        place_ref[pl.ds(start, half), :] = hit.astype(jnp.bfloat16)
+        place_ref[pl.ds(start, half), :] = jnp.where(
+            outer == jnp.bfloat16(chunk), inner, jnp.bfloat16(0.0)
+        )
 
     def add_tile(tile, held):
         lanes = slice(tile * LANES, (tile + 1) * LANES)
@@ -612,7 +620,7 @@
         near = jnp.where(upper, before, after)
         far = opposite_class(jnp.where(upper, after, before), lane)
         for inner in range(4):
-            at = (brick * 4 + inner) * BLOCK_ROWS
+            at = block_of(brick, inner, bricks) * BLOCK_ROWS
             edge = jnp.where(near_lanes(lane, inner // 2, inner % 2), near, far)
             send_ref[at : at + SUM_ROWS, :] = own_sums[brick][0:SUM_ROWS]
             send_ref[at + SUM_ROWS : at + FIELD_AT, :] = edge[0:EDGE_ROWS]
@@ -633,17 +641,24 @@
     return list(terms.items())
 
 
+def tree_sum(terms):
+    while len(terms) > 1:
+        paired = [one + two for one, two in zip(terms[0::2], terms[1::2])]
+        terms = paired + terms[2 * len(paired) :]
+    return terms[0]
+
+
 def plane_derivative(field, shifts):
-    return ordered_sum([weights * pltpu.roll(field, shift, 1) for shift, weights in shifts])
+    return tree_sum([weights * pltpu.roll(field, shift, 1) for shift, weights in shifts])
 
 
 def row_derivative(read, start, count):
-    total = stencil_weights[0] * (read(start + 1, count) - read(start - 1, count))
-    for order in range(2, 5):
-        total = total + stencil_weights[order - 1] * (
-            read(start + order, count) - read(start - order, count)
-        )
-    return total
+    return tree_sum(
+        [
+            stencil_weights[order - 1] * (read(start + order, count) - read(start - order, count))
+            for order in range(1, 5)
+        ]
+    )
 
 
 def velocity_update(wide_stress, old_velocity, density, inside, count):
@@ -688,7 +703,7 @@
     return [
         old_stress[row]
         + time_step
-        * ordered_sum([stiff(symmetric_index(row, col)) * strain[col] for col in range(6)])
+        * tree_sum([stiff(symmetric_index(row, col)) * strain[col] for col in range(6)])
         for row in range(6)
     ]
 
@@ -712,8 +727,10 @@
     for p in range(bricks):
 
         def both_layers(part, offset, count):
-            at = (p * 4 + part * 2) * BLOCK_ROWS + offset
-            return got_ref[at : at + count, :] + got_ref[at + BLOCK_ROWS : at + BLOCK_ROWS + count, :]
+            first, second = [
+                block_of(p, part * 2 + layer, bricks) * BLOCK_ROWS + offset for layer in range(2)
+            ]
+            return got_ref[first : first + count, :] + got_ref[second : second + count, :]
 
         low, high = by_slot(both_layers(0, 0, SUM_ROWS), both_layers(1, 0, SUM_ROWS))
         total = jnp.broadcast_to(high[10:11], (SUB, LANES))
@@ -732,7 +749,7 @@
         lane = lanes_of((count, LANES))
         kind = (lane // 64) * 2 + (lane // 8) % 2
         pieces = [
-            got_ref[pl.ds((source * 4 + (q ^ slot)) * BLOCK_ROWS + offset, count), :]
+            got_ref[pl.ds(block_of(source, q ^ slot, bricks) * BLOCK_ROWS + offset, count), :]
             for q in range(4)
         ]
         value = jnp.where(
@@ -904,7 +921,7 @@
     )])
     got = lax.all_to_all(
         send.reshape(devices, 1, BLOCK_ROWS * LANES),
-        ("gx", "gy", "ga"),
+        ("ga", "gx", "gy"),
         split_axis=0,
         concat_axis=0,
         tiled=True,

time: 28.5 us -> 27.9 us (0.979)
  blocking collectives: 21.7 us -> 21.3 us
    all_to_all x1, blocking collectives: 21.7 us -> 21.3 us  [on_plane(): lax.all_to_all(send.reshape(devices, 1, BLOCK_ROWS * LANES), ('ga', 'gx',...]
where the time goes in v7:
time: 27.9 us; the launch traced here: 27.8 us
  blocking collectives  21.3 us (76%)
  Pallas kernels  5.1 us (18%)
  waiting for transfers between devices  0.69 us (2%)
  between operations  0.66 us (2%)
    all_to_all x1, blocking collectives, on_plane(): lax.all_to_all(send.reshape(devices, 1, BLOCK_ROWS * LANES), ('ga', 'gx',...  21.3 us
    pallas_call x1, Pallas kernels, on_plane(): pl.pallas_call(grain_kernel, out_shape=jax.ShapeDtypeStruct((devices * BL...  2.35 us
    pallas_call x1, Pallas kernels, on_plane(): pl.pallas_call(functools.partial(steps_kernel, bricks=part_x), out_shape=...  1.64 us
    pallas_call x1, Pallas kernels, on_plane(): pl.pallas_call(stiffness_kernel, out_shape=jax.ShapeDtypeStruct((SUB * 4...  0.87 us
    ppermute x1, waiting for transfers between devices, on_plane(): lax.ppermute(own_part, 'gx', [(i, i ^ 1) for i in range(part_x)])  0.69 us
  transfers between devices with their start and end apart: 1, of which 1 were waited for; matrix products, arithmetic and copies ran while one was open for 0% of the time, Pallas kernels for 3%

profile of v7, /device:TPU:0, one launch (start us, length us, event | category | flops | bytes accessed | tf_op | source)
XLA Modules:
  0.0 27.8 jit_solution(4896037346672060948)
XLA Ops:
  0.6 2.3 %shard_map.103 = f32[864,128]{1,0:T(8,128)S(1)} custom-call(f32[21]{0:T(128)} %crystal_hbm.1, f32[3,2048]{1,0:T(4,128)} %euler_hbm.1, s32[64,128]{1,0:T(8,128)} %bitcast.18, bf16[16,512]{1,0:T(8,128)(2,1)} %bitcast.19, s32[1,512]{1,0:T(1,128)} %bitcast.21, f32[32,8]{1,0:T(8,128)} %bitcast.20, f32[96,8]{1,0:T(8,128)} %bitcast.17, f32[192,8]{1,0:T(8,128)} %bitcast.16), custom_call_target="tpu_custom_call" | custom-call | tf_op jit(solution)/shard_map/pallas_call | solution.py:891
  3.0 21.3 %all_to_all.5 = f32[32,1,3456]{2,1,0:T(1,128)S(1)} all-to-all(f32[32,1,3456]{2,1,0:T(1,128)S(1)} %bitcast.13), channel_id=1, replica_groups=mesh['gx'=8,'gy'=2,'ga'=2] {'ga','gx','gy'}, dimensions={0} | all-to-all | bytes 884736 | tf_op jit(solution)/shard_map/all_to_all | solution.py:922
  24.3 0.2 shard_map.104.stiff_ref.own_ref
  24.5 0.1 collective-permute-start
  24.6 0.9 %shard_map.105 = f32[256,21]{1,0:T(8,128)} custom-call(f32[560,128]{1,0:T(8,128)S(1)} %shard_map.104.stiff_ref.own_ref), custom_call_target="tpu_custom_call" | custom-call | flops 100000 | bytes 200000 | tf_op jit(solution)/shard_map/pallas_call | solution.py:938
  25.5 0.7 %collective-permute-done.other_ref = f32[560,128]{1,0:T(8,128)S(1)} collective-permute-done((f32[560,128]{1,0:T(8,128)S(1)}, f32[560,128]{1,0:T(8,128)S(1)}, u32[]{:S(2)}, u32[]{:S(2)}) %collective-permute-start) | collective-permute-done | bytes 286752 | tf_op jit(solution)/shard_map/ppermute | solution.py:937
  26.1 1.6 %shard_map.106 = (f32[96,8]{1,0:T(8,128)}, f32[192,8]{1,0:T(8,128)}) custom-call(f32[560,128]{1,0:T(8,128)S(1)} %shard_map.104.stiff_ref.own_ref, f32[560,128]{1,0:T(8,128)S(1)} %collective-permute-done.other_ref), custom_call_target="tpu_custom_call" | custom-call | tf_op jit(solution)/shard_map/pallas_call | solution.py:947
Async XLA Ops:
  24.5 1.6 %collective-permute-start = (f32[560,128]{1,0:T(8,128)S(1)}, f32[560,128]{1,0:T(8,128)S(1)}, u32[]{:S(2)}, u32[]{:S(2)}) collective-permute-start(f32[560,128]{1,0:T(8,128)S(1)} %shard_map.104.stiff_ref.own_ref), channel_id=1, source_target_pairs={{0,4},{4,0},{8,12},{12,8},{16,20},{20,16},{24,28},{28,24},{1,5},{5... | collective-permute-start | bytes 860168 | tf_op jit(solution)/shard_map/ppermute | solution.py:937

commit v8 on v7

--- a/solution.py
+++ b/solution.py
@@ -226,8 +226,9 @@
 EDGE_ROWS = 6
 FIELD_AT = SUM_ROWS + EDGE_ROWS
 BLOCK_ROWS = FIELD_AT + 10
-EDGE_AT = 192
-WIDE_AT = EDGE_AT + 128
+STIFF_ROWS = 22
+EDGE_AT = STIFF_ROWS * SUB
+WIDE_AT = EDGE_AT + SUM_ROWS * SUB
 WIDE_ROWS = 48
 FIELDS = 10
 HALF = FIELDS // 2
@@ -466,10 +467,10 @@
         pltpu.make_async_copy(source, target, arrived.at[at])
         for at, (source, target) in enumerate(
             [
+                (map_hbm, map_ref),
+                (crystal_hbm, crystal_ref),
                 (orient_hbm, orient_ref),
                 (euler_hbm, euler_ref),
-                (map_hbm, map_ref),
-                (crystal_hbm, crystal_ref),
                 (weight_hbm, weight_ref),
                 (stress_hbm, stress_ref),
                 (velocity_hbm, velocity_ref),
@@ -734,14 +735,15 @@
 
         low, high = by_slot(both_layers(0, 0, SUM_ROWS), both_layers(1, 0, SUM_ROWS))
         total = jnp.broadcast_to(high[10:11], (SUB, LANES))
-        out_ref[p * 24 : p * 24 + 8, :] = low[0:8] / total
-        out_ref[p * 24 + 8 : p * 24 + 16, :] = high[0:8] / total
-        out_ref[p * 24 + 16 : p * 24 + 19, :] = low[8:11] / total[0:3]
-        out_ref[p * 24 + 19 : p * 24 + 22, :] = high[8:11] / total[0:3]
+        at = p * STIFF_ROWS
+        out_ref[at : at + 8, :] = low[0:8] / total
+        out_ref[at + 8 : at + 16, :] = high[0:8] / total
+        out_ref[at + 16 : at + 19, :] = low[8:11] / total[0:3]
+        out_ref[at + 19 : at + 22, :] = high[8:11] / total[0:3]
         low, high = by_slot(
             both_layers(0, SUM_ROWS, EDGE_ROWS), both_layers(1, SUM_ROWS, EDGE_ROWS)
         )
-        at = EDGE_AT + p * 16
+        at = EDGE_AT + p * SUM_ROWS
         out_ref[at : at + EDGE_ROWS, :] = low
         out_ref[at + EDGE_ROWS : at + SUM_ROWS, :] = high[0 : SUM_ROWS - EDGE_ROWS]
 
@@ -783,7 +785,7 @@
 def stiffness_kernel(stiff_ref, out_ref, turned_ref):
     own = lax.axis_index("gy") * 64 + lax.axis_index("ga") * 8
     for p in range(SUB):
-        turned_ref[...] = jnp.transpose(stiff_ref[p * 24 : (p + 1) * 24, :])
+        turned_ref[...] = jnp.transpose(stiff_ref[p * STIFF_ROWS : p * STIFF_ROWS + 24, :])
         for y in range(4):
             rows = pl.ds(pl.multiple_of(own + y * 16, 8), 8)
             out_ref[p * 32 + y * 8 : p * 32 + y * 8 + 8, :] = turned_ref[rows, 0:21]
@@ -820,7 +822,7 @@
     usable = (own_lane | (near_row & near_lanes(lane, row_part, layer))) & edge_valid
 
     def edge(half, k):
-        rows = pl.ds(EDGE_AT + k, SUB, stride=16)
+        rows = pl.ds(EDGE_AT + k, SUB, stride=SUM_ROWS)
         value = jnp.where(odd == half, own_ref[rows, :], other_ref[rows, :])
         return jnp.where(near_row, value, opposite_class(value, lane))
 
@@ -837,10 +839,10 @@
     )
     for at in range(3):
         first_velocity_ref[at] = fresh[at]
-    own_stiff = lambda pair: own_ref[pl.ds(pair, SUB, stride=24), :]
+    own_stiff = lambda pair: own_ref[pl.ds(pair, SUB, stride=STIFF_ROWS), :]
     for group, stiff, valid in (
         (SUB, own_stiff, None),
-        (2 * SUB - odd * 2 * SUB, lambda pair: other_ref[pl.ds(pair, SUB, stride=24), :], None),
+        (2 * SUB - odd * 2 * SUB, lambda pair: other_ref[pl.ds(pair, SUB, stride=STIFF_ROWS), :], None),
         (odd * 2 * SUB, lambda pair: edge_ref[pair], edge_valid),
     ):
         fresh = stress_update(

time: 27.9 us -> 27.9 us (level)
  no operation moved by 1% of the time
where the time goes in v8:
time: 27.9 us; the launch traced here: 27.7 us
  blocking collectives  21.3 us (76%)
  Pallas kernels  5.08 us (18%)
  between operations  0.66 us (2%)
  waiting for transfers between devices  0.64 us (2%)
    all_to_all x1, blocking collectives, on_plane(): lax.all_to_all(send.reshape(devices, 1, BLOCK_ROWS * LANES), ('ga', 'gx',...  21.3 us
    pallas_call x1, Pallas kernels, on_plane(): pl.pallas_call(grain_kernel, out_shape=jax.ShapeDtypeStruct((devices * BL...  2.34 us
    pallas_call x1, Pallas kernels, on_plane(): pl.pallas_call(functools.partial(steps_kernel, bricks=part_x), out_shape=...  1.63 us
    pallas_call x1, Pallas kernels, on_plane(): pl.pallas_call(stiffness_kernel, out_shape=jax.ShapeDtypeStruct((SUB * 4...  0.87 us
    ppermute x1, waiting for transfers between devices, on_plane(): lax.ppermute(own_part, 'gx', [(i, i ^ 1) for i in range(part_x)])  0.64 us
  transfers between devices with their start and end apart: 1, of which 1 were waited for; matrix products, arithmetic and copies ran while one was open for 0% of the time, Pallas kernels for 3%

profile of v8, /device:TPU:0, one launch (start us, length us, event | category | flops | bytes accessed | tf_op | source)
XLA Modules:
  0.0 27.7 jit_solution(15973405868368190461)
XLA Ops:
  0.6 2.3 %shard_map.103 = f32[864,128]{1,0:T(8,128)S(1)} custom-call(f32[21]{0:T(128)} %crystal_hbm.1, f32[3,2048]{1,0:T(4,128)} %euler_hbm.1, s32[64,128]{1,0:T(8,128)} %bitcast.18, bf16[16,512]{1,0:T(8,128)(2,1)} %bitcast.19, s32[1,512]{1,0:T(1,128)} %bitcast.21, f32[32,8]{1,0:T(8,128)} %bitcast.20, f32[96,8]{1,0:T(8,128)} %bitcast.17, f32[192,8]{1,0:T(8,128)} %bitcast.16), custom_call_target="tpu_custom_call" | custom-call | tf_op jit(solution)/shard_map/pallas_call | solution.py:893
  3.0 21.3 %all_to_all.5 = f32[32,1,3456]{2,1,0:T(1,128)S(1)} all-to-all(f32[32,1,3456]{2,1,0:T(1,128)S(1)} %bitcast.13), channel_id=1, replica_groups=mesh['gx'=8,'gy'=2,'ga'=2] {'ga','gx','gy'}, dimensions={0} | all-to-all | bytes 884736 | tf_op jit(solution)/shard_map/all_to_all | solution.py:924
  24.2 0.2 shard_map.104.stiff_ref.own_ref
  24.5 0.1 collective-permute-start
  24.6 0.9 %shard_map.105 = f32[256,21]{1,0:T(8,128)} custom-call(f32[504,128]{1,0:T(8,128)S(1)} %shard_map.104.stiff_ref.own_ref), custom_call_target="tpu_custom_call" | custom-call | flops 100000 | bytes 200000 | tf_op jit(solution)/shard_map/pallas_call | solution.py:940
  25.4 0.6 %collective-permute-done.other_ref = f32[504,128]{1,0:T(8,128)S(1)} collective-permute-done((f32[504,128]{1,0:T(8,128)S(1)}, f32[504,128]{1,0:T(8,128)S(1)}, u32[]{:S(2)}, u32[]{:S(2)}) %collective-permute-start) | collective-permute-done | bytes 258080 | tf_op jit(solution)/shard_map/ppermute | solution.py:939
  26.1 1.6 %shard_map.106 = (f32[96,8]{1,0:T(8,128)}, f32[192,8]{1,0:T(8,128)}) custom-call(f32[504,128]{1,0:T(8,128)S(1)} %shard_map.104.stiff_ref.own_ref, f32[504,128]{1,0:T(8,128)S(1)} %collective-permute-done.other_ref), custom_call_target="tpu_custom_call" | custom-call | tf_op jit(solution)/shard_map/pallas_call | solution.py:949
Async XLA Ops:
  24.5 1.6 %collective-permute-start = (f32[504,128]{1,0:T(8,128)S(1)}, f32[504,128]{1,0:T(8,128)S(1)}, u32[]{:S(2)}, u32[]{:S(2)}) collective-permute-start(f32[504,128]{1,0:T(8,128)S(1)} %shard_map.104.stiff_ref.own_ref), channel_id=1, source_target_pairs={{0,4},{4,0},{8,12},{12,8},{16,20},{20,16},{24,28},{28,24},{1,5},{5... | collective-permute-start | bytes 774152 | tf_op jit(solution)/shard_map/ppermute | solution.py:939

commit v9 on v8

--- a/solution.py
+++ b/solution.py
@@ -290,7 +290,7 @@
 
 
 def block_of(brick, inner, bricks):
-    return (inner % 2) * bricks * 2 + brick * 2 + inner // 2
+    return (inner // 2) * bricks * 2 + brick * 2 + inner % 2
 
 
 def near_lanes(lane, row_half, layer):
@@ -923,7 +923,7 @@
     )])
     got = lax.all_to_all(
         send.reshape(devices, 1, BLOCK_ROWS * LANES),
-        ("ga", "gx", "gy"),
+        ("gy", "gx", "ga"),
         split_axis=0,
         concat_axis=0,
         tiled=True,

time: 27.9 us -> 27.9 us (level)
  no operation moved by 1% of the time
where the time goes in v9:
time: 27.9 us; the launch traced here: 27.7 us
  blocking collectives  21.2 us (76%)
  Pallas kernels  5.08 us (18%)
  between operations  0.66 us (2%)
  waiting for transfers between devices  0.64 us (2%)
    all_to_all x1, blocking collectives, on_plane(): lax.all_to_all(send.reshape(devices, 1, BLOCK_ROWS * LANES), ('gy', 'gx',...  21.2 us
    pallas_call x1, Pallas kernels, on_plane(): pl.pallas_call(grain_kernel, out_shape=jax.ShapeDtypeStruct((devices * BL...  2.34 us
    pallas_call x1, Pallas kernels, on_plane(): pl.pallas_call(functools.partial(steps_kernel, bricks=part_x), out_shape=...  1.63 us
    pallas_call x1, Pallas kernels, on_plane(): pl.pallas_call(stiffness_kernel, out_shape=jax.ShapeDtypeStruct((SUB * 4...  0.87 us
    ppermute x1, waiting for transfers between devices, on_plane(): lax.ppermute(own_part, 'gx', [(i, i ^ 1) for i in range(part_x)])  0.64 us
  transfers between devices with their start and end apart: 1, of which 1 were waited for; matrix products, arithmetic and copies ran while one was open for 0% of the time, Pallas kernels for 3%

profile of v9, /device:TPU:0, one launch (start us, length us, event | category | flops | bytes accessed | tf_op | source)
XLA Modules:
  0.0 27.7 jit_solution(6492874460490692031)
XLA Ops:
  0.6 2.3 %shard_map.103 = f32[864,128]{1,0:T(8,128)S(1)} custom-call(f32[21]{0:T(128)} %crystal_hbm.1, f32[3,2048]{1,0:T(4,128)} %euler_hbm.1, s32[64,128]{1,0:T(8,128)} %bitcast.18, bf16[16,512]{1,0:T(8,128)(2,1)} %bitcast.19, s32[1,512]{1,0:T(1,128)} %bitcast.21, f32[32,8]{1,0:T(8,128)} %bitcast.20, f32[96,8]{1,0:T(8,128)} %bitcast.17, f32[192,8]{1,0:T(8,128)} %bitcast.16), custom_call_target="tpu_custom_call" | custom-call | tf_op jit(solution)/shard_map/pallas_call | solution.py:893
  3.0 21.2 %all_to_all.5 = f32[32,1,3456]{2,1,0:T(1,128)S(1)} all-to-all(f32[32,1,3456]{2,1,0:T(1,128)S(1)} %bitcast.13), channel_id=1, replica_groups=mesh['gx'=8,'gy'=2,'ga'=2] {'gy','gx','ga'}, dimensions={0} | all-to-all | bytes 884736 | tf_op jit(solution)/shard_map/all_to_all | solution.py:924
  24.2 0.2 shard_map.104.stiff_ref.own_ref
  24.5 0.1 collective-permute-start
  24.6 0.9 %shard_map.105 = f32[256,21]{1,0:T(8,128)} custom-call(f32[504,128]{1,0:T(8,128)S(1)} %shard_map.104.stiff_ref.own_ref), custom_call_target="tpu_custom_call" | custom-call | flops 100000 | bytes 200000 | tf_op jit(solution)/shard_map/pallas_call | solution.py:940
  25.4 0.6 %collective-permute-done.other_ref = f32[504,128]{1,0:T(8,128)S(1)} collective-permute-done((f32[504,128]{1,0:T(8,128)S(1)}, f32[504,128]{1,0:T(8,128)S(1)}, u32[]{:S(2)}, u32[]{:S(2)}) %collective-permute-start) | collective-permute-done | bytes 258080 | tf_op jit(solution)/shard_map/ppermute | solution.py:939
  26.1 1.6 %shard_map.106 = (f32[96,8]{1,0:T(8,128)}, f32[192,8]{1,0:T(8,128)}) custom-call(f32[504,128]{1,0:T(8,128)S(1)} %shard_map.104.stiff_ref.own_ref, f32[504,128]{1,0:T(8,128)S(1)} %collective-permute-done.other_ref), custom_call_target="tpu_custom_call" | custom-call | tf_op jit(solution)/shard_map/pallas_call | solution.py:949
Async XLA Ops:
  24.5 1.6 %collective-permute-start = (f32[504,128]{1,0:T(8,128)S(1)}, f32[504,128]{1,0:T(8,128)S(1)}, u32[]{:S(2)}, u32[]{:S(2)}) collective-permute-start(f32[504,128]{1,0:T(8,128)S(1)} %shard_map.104.stiff_ref.own_ref), channel_id=1, source_target_pairs={{0,4},{4,0},{8,12},{12,8},{16,20},{20,16},{24,28},{28,24},{1,5},{5... | collective-permute-start | bytes 774152 | tf_op jit(solution)/shard_map/ppermute | solution.py:939
